TPU v7x, 512 devices: a whole 4x4x16 slice. The times are simulated.
512 devices in a mesh: inst: 16 (over z), mesh: 32 (over y, x, core).
Axes of the slice: x: 4, y: 4, z: 16, core: 2. Of those that a mesh axis runs over, the one named last changes fastest.
Arguments:
- state: float32 [16, 6, 2048, 128], P('inst', None, 'mesh'), may hold values from -6 to 6
- right_side: float32 [16, 6, 2048, 128], P('inst', None, 'mesh'), may hold values from -6 to 6
- couplings: float32 [3, 16, 6, 2048, 128], P(None, 'inst', None, 'mesh'), may hold values from 0.05 to 0.35
- jac_corr: float32 [16, 6, 6, 2048, 128], P('inst', None, None, 'mesh'), may hold values from -0.3 to 0.3
- spec_scale: float32 [2048, 128], P('mesh'), may hold values from 0.005 to 0.05
- row_id: int32 [2048], P('mesh'), may hold values from 0 to 2
- send_index: int32 [1024, 2], P('mesh'), may hold values from 0 to 63
- recv_slot: int32 [2048], P('mesh'), may hold values from 0 to 63, as said below
- iface_coef: float32 [64, 128], P('mesh'), may hold values from 0.2 to 0.6
- donor_index: int32 [64, 2], P('mesh'), may hold values from 0 to 63
- donor_weight: float32 [64, 2], P('mesh'), may hold values from 0.2 to 1
- phase_shift: int32 [64], P('mesh'), may hold values from 0 to 15
Outputs:
- smoothed: float32 [16, 6, 2048, 128], P('inst', None, 'mesh')
Inputs may be any that keep to these rules, and one draw needn't show every extreme that they name: `recv_slot`: among the 64 blocks of each mesh index, every slot 0 to 32 * 2 - 1 is named by at least one block.
All inputs are finite; a program needn't handle non-finite values.
Results may differ from a plain program's by a relative error of at most 0.0001.
Values sent between devices are 32-bit elements; how exact they have to be, the bound alone decides.
No kernel may reach another device: no remote copies, remote signals or barrier semaphores. Data moves between devices by JAX's collectives and lax.ppermute only.
A program may use at most 64 MiB of HBM per device.

v0:
```python
import jax
import jax.numpy as jnp
from jax import lax
from jax.sharding import PartitionSpec as P

NT = 16
NV = 6
BLOCK_CELLS = 128
SWEEPS = 2


def from_everyone(shard, axis):
    length = lax.axis_size(axis)
    return lax.all_to_all(
        jnp.broadcast_to(shard[None], (length, *shard.shape)), axis, 0, 0, tiled=True
    )


def laid_out(blocks, dim):
    lengths = list(blocks.shape[1:])
    lengths[dim] *= blocks.shape[0]
    return jnp.moveaxis(blocks, 0, dim).reshape(lengths)


def gather_directly(shard, axis, dim):
    blocks = from_everyone(shard, axis)
    return laid_out(blocks, dim)


def spectral_table(length):
    row_ids = jnp.arange(length)[:, None]
    col_ids = jnp.arange(length)[None, :]
    offsets = row_ids - col_ids
    parity = 1.0 - 2.0 * (offsets % 2).astype(jnp.float32)
    angles = jnp.pi * offsets.astype(jnp.float32) / length
    on_diag = offsets == 0
    sine_safe = jnp.where(on_diag, 1.0, jnp.sin(angles))
    first = jnp.where(on_diag, 0.0, 0.5 * parity * jnp.cos(angles) / sine_safe)
    diag_value = -(length * length + 2.0) / 12.0
    second = jnp.where(on_diag, diag_value, -0.5 * parity / (sine_safe * sine_safe))
    return first - 0.1 * second


def line_terms(field, couplings):
    zeros_col = jnp.zeros_like(field[..., :1])
    below = jnp.concatenate([zeros_col, field[..., :-1]], axis=-1)
    above = jnp.concatenate([field[..., 1:], zeros_col], axis=-1)
    return couplings[0] * below + couplings[1] * above


def jacobi_update(total_rhs, jac_corr):
    updated = 0.35 * total_rhs + jnp.einsum(
        "nvwbc,nwbc->nvbc", jac_corr, total_rhs, precision=lax.Precision.HIGHEST
    )
    return updated.at[:, -1].set(jnp.maximum(updated[:, -1], 0.0))


def donor_mix(donor_pool, donor_index, donor_weight):
    first_part = donor_pool[:, :, donor_index[:, 0]] * donor_weight[:, 0][:, None]
    second_part = donor_pool[:, :, donor_index[:, 1]] * donor_weight[:, 1][:, None]
    return first_part + second_part


def phase_pick(combined, shift_src):
    targets = jnp.arange(combined.shape[2])[None, :]
    picked = combined[shift_src, :, targets]
    return jnp.transpose(picked, (0, 2, 1, 3))


def per_device(
    state,
    right_side,
    couplings,
    jac_corr,
    spec_scale,
    row_id,
    send_index,
    recv_slot,
    iface_coef,
    donor_index,
    donor_weight,
    phase_shift,
):
    table = spectral_table(NT)
    local_inst = state.shape[0]
    iface_local = iface_coef.shape[0]
    first_inst = lax.axis_index("inst") * local_inst
    own_rows = lax.dynamic_slice_in_dim(table, first_inst, local_inst, 0)
    row_factor = 1.0 + 0.5 * row_id.astype(jnp.float32)
    frequency = spec_scale * row_factor[:, None]
    shift_src = (first_inst + jnp.arange(local_inst)[:, None] + phase_shift[None, :]) % NT
    field = state
    for sweep_index in range(SWEEPS):
        spectral = jnp.einsum(
            "nm,mvbc->nvbc",
            own_rows,
            lax.all_gather(field, "inst", axis=0, tiled=True),
            precision=lax.Precision.HIGHEST,
        )
        outgoing = field[:, :, send_index]
        incoming = lax.all_to_all(outgoing, "mesh", split_axis=2, concat_axis=2, tiled=True)
        incoming = incoming.reshape(local_inst, NV, -1, BLOCK_CELLS)
        halo_vals = incoming[:, :, recv_slot]
        faces = field[:, :, :iface_local]
        donor_pool = gather_directly(faces, "mesh", 2)
        local_mix = donor_mix(donor_pool, donor_index, donor_weight)
        combined = gather_directly(local_mix, "inst", 0)
        iface_term = iface_coef * phase_pick(combined, shift_src)
        total_rhs = (
            right_side
            + line_terms(field, couplings)
            + couplings[2] * halo_vals
            - frequency * spectral
        )
        total_rhs = total_rhs.at[:, :, :iface_local].add(iface_term)
        field = jacobi_update(total_rhs, jac_corr)
    return field


def solution(mesh):
    return jax.shard_map(
        per_device,
        mesh=mesh,
        in_specs=(
            P("inst", None, "mesh", None),
            P("inst", None, "mesh", None),
            P(None, "inst", None, "mesh", None),
            P("inst", None, None, "mesh", None),
            P("mesh", None),
            P("mesh"),
            P("mesh", None),
            P("mesh"),
            P("mesh", None),
            P("mesh", None),
            P("mesh", None),
            P("mesh"),
        ),
        out_specs=P("inst", None, "mesh", None),
        check_vma=False,
    )
```

profile of v0, /device:TPU:6, one launch (start us, length us, event | category | flops | bytes accessed | tf_op | source)
XLA Modules:
  0.0 188.5 jit_solution(6862452130185277120)
XLA Ops:
  6.5 0.7 all-gather.3.cloned.1.call-update
  7.3 0.7 slice_bitcast_fusion.1
  8.0 0.7 broadcast_in_dim.31
  8.7 9.4 %all-to-all-start.1 = ((f32[32,1,6,2,128]{4,3,2,1,0:T(2,128)}), f32[32,1,6,2,128]{4,3,2,1,0:T(2,128)S(1)}, u32[]{:S(2)}, u32[]{:S(2)}) async-start(f32[32,1,6,2,128]{4,3,2,1,0:T(2,128)} %broadcast_in_dim.31), calls=%async_computation.1 | async-start | bytes 393216 | tf_op jit(solution)/shard_map/all_to_all | solution.py:14
  18.1 1.1 copy.147
  19.2 0.7 fusion.36
  20.0 0.7 compare_select_fusion.2
  20.8 0.6 gather_fusion
  21.5 0.8 copy.144
  22.3 0.7 compare_select_fusion.4
  22.9 1.0 slice_reduce_fusion.1
  24.0 1.0 fusion.28
  24.9 0.2 or_reduce_fusion
  25.1 0.7 multiply_add_fusion
  25.8 1.1 fusion.41
  26.9 0.8 broadcast_multiply_fusion
  27.8 7.5 %all-to-all-start = ((f32[1,6,32,2,128]{4,3,1,0,2:T(2,128)}), f32[1,6,32,2,128]{4,3,1,0,2:T(2,128)S(1)}, u32[]{:S(2)}, u32[]{:S(2)}) async-start(f32[1,6,32,2,128]{4,3,1,0,2:T(2,128)} %bitcast.137), calls=%async_computation | async-start | bytes 393216 | tf_op jit(solution)/shard_map/all_to_all | solution.py:101
  35.5 0.5 gather_fusion.3
  36.0 0.5 gather_fusion.2
  36.7 5.2 %all-to-all-done = f32[1,6,32,2,128]{4,3,1,0,2:T(2,128)S(1)} async-done(((f32[1,6,32,2,128]{4,3,1,0,2:T(2,128)}), f32[1,6,32,2,128]{4,3,1,0,2:T(2,128)S(1)}, u32[]{:S(2)}, u32[]{:S(2)}) %all-to-all-start) | async-done | bytes 196640 | tf_op jit(solution)/shard_map/all_to_all | solution.py:101
  41.8 0.7 broadcast_in_dim.32
  42.5 13.3 %all-to-all-start.2 = ((f32[16,1,6,2,128]{4,3,2,1,0:T(2,128)}), f32[16,1,6,2,128]{4,3,2,1,0:T(2,128)S(1)}, u32[]{:S(2)}, u32[]{:S(2)}) async-start(f32[16,1,6,2,128]{4,3,2,1,0:T(2,128)} %broadcast_in_dim.32), calls=%async_computation.2 | async-start | bytes 196608 | tf_op jit(solution)/shard_map/all_to_all | solution.py:14
  56.3 0.6 gather_fusion.1
  56.9 13.0 %all-to-all-done.2 = f32[16,1,6,2,128]{4,3,2,1,0:T(2,128)S(1)} async-done(((f32[16,1,6,2,128]{4,3,2,1,0:T(2,128)}), f32[16,1,6,2,128]{4,3,2,1,0:T(2,128)S(1)}, u32[]{:S(2)}, u32[]{:S(2)}) %all-to-all-start.2) | async-done | bytes 98336 | tf_op jit(solution)/shard_map/all_to_all | solution.py:14
  70.0 0.6 gather_fusion.4
  70.5 22.1 %all-gather.3.cloned.1.call-done = f32[16,6,64,128]{3,2,1,0:T(8,128)} async-done(((f32[1,6,64,128]{3,2,1,0:T(8,128)}), f32[16,6,64,128]{3,2,1,0:T(8,128)}) %all-gather.3.cloned.1.call-update) | async-done | bytes 3145744 | tf_op jit(solution)/shard_map/all_gather | solution.py:97
  92.7 5.1 %fusion.2 = f32[1,6,64,128]{3,0,2,1:T(1,128)S(1)} fusion(f32[16,6,64,128]{3,2,1,0:T(8,128)} %all-gather.3.cloned.1.call-done, pred[16,16]{1,0:T(8,128)(4,1)S(1)} %fusion.23, s32[]{:T(128)S(6)} %select_n.58, f32[16,16]{1,0:T(8,128)S(1)} %get-tuple-element.65, f32[16,16]{1,0:T(8,128)S(1)} %fusion.27, f32[16,16]{1,0:T(8,128)S(1)} %get-tuple-element.64), kind=kOutput, calls=%fused_computation.12 | convolution fusion | flops 9437376 | bytes 3344388 | tf_op jit(solution)/shard_map/nm,mvbc->nvbc/dot_general | solution.py:94
  97.8 0.6 fusion.9
  98.8 0.1 scatter.6
  99.0 0.7 copy.50
  99.7 0.7 broadcast_in_dim.35
  100.5 6.8 %all-to-all-start.4 = ((f32[32,1,6,2,128]{4,3,2,1,0:T(2,128)}), f32[32,1,6,2,128]{4,3,2,1,0:T(2,128)S(1)}, u32[]{:S(2)}, u32[]{:S(2)}) async-start(f32[32,1,6,2,128]{4,3,2,1,0:T(2,128)} %broadcast_in_dim.35), calls=%async_computation.4 | async-start | bytes 393216 | tf_op jit(solution)/shard_map/all_to_all | solution.py:14
  107.3 0.6 gather_fusion.5
  107.9 0.8 copy.143
  108.7 5.2 %all-to-all-done.4 = f32[32,1,6,2,128]{4,3,2,1,0:T(2,128)S(1)} async-done(((f32[32,1,6,2,128]{4,3,2,1,0:T(2,128)}), f32[32,1,6,2,128]{4,3,2,1,0:T(2,128)S(1)}, u32[]{:S(2)}, u32[]{:S(2)}) %all-to-all-start.4) | async-done | bytes 196640 | tf_op jit(solution)/shard_map/all_to_all | solution.py:14
  113.8 5.5 %all-to-all-start.3 = ((f32[1,6,32,2,128]{4,3,1,0,2:T(2,128)}), f32[1,6,32,2,128]{4,3,1,0,2:T(2,128)S(1)}, u32[]{:S(2)}, u32[]{:S(2)}) async-start(f32[1,6,32,2,128]{4,3,1,0,2:T(2,128)} %bitcast.136), calls=%async_computation.3 | async-start | bytes 393216 | tf_op jit(solution)/shard_map/all_to_all | solution.py:101
  119.5 0.5 gather_fusion.8
  120.1 0.5 gather_fusion.7
  120.7 5.2 %all-to-all-done.3 = f32[1,6,32,2,128]{4,3,1,0,2:T(2,128)S(1)} async-done(((f32[1,6,32,2,128]{4,3,1,0,2:T(2,128)}), f32[1,6,32,2,128]{4,3,1,0,2:T(2,128)S(1)}, u32[]{:S(2)}, u32[]{:S(2)}) %all-to-all-start.3) | async-done | bytes 196640 | tf_op jit(solution)/shard_map/all_to_all | solution.py:101
  125.9 0.7 broadcast_in_dim.36
  126.6 7.5 %all-to-all-start.5 = ((f32[16,1,6,2,128]{4,3,2,1,0:T(2,128)}), f32[16,1,6,2,128]{4,3,2,1,0:T(2,128)S(1)}, u32[]{:S(2)}, u32[]{:S(2)}) async-start(f32[16,1,6,2,128]{4,3,2,1,0:T(2,128)} %broadcast_in_dim.36), calls=%async_computation.5 | async-start | bytes 196608 | tf_op jit(solution)/shard_map/all_to_all | solution.py:14
  134.2 0.6 gather_fusion.6
  134.9 13.6 %all-to-all-done.5 = f32[16,1,6,2,128]{4,3,2,1,0:T(2,128)S(1)} async-done(((f32[16,1,6,2,128]{4,3,2,1,0:T(2,128)}), f32[16,1,6,2,128]{4,3,2,1,0:T(2,128)S(1)}, u32[]{:S(2)}, u32[]{:S(2)}) %all-to-all-start.5) | async-done | bytes 98336 | tf_op jit(solution)/shard_map/all_to_all | solution.py:14
  148.4 0.6 gather_fusion.9
  149.0 25.7 %all-gather.5.cloned.1.call-done = f32[16,6,64,128]{3,2,1,0:T(8,128)} async-done(((f32[1,6,64,128]{3,2,1,0:T(8,128)}), f32[16,6,64,128]{3,2,1,0:T(8,128)}) %all-gather.5.cloned.1.call-update) | async-done | bytes 3145744 | tf_op jit(solution)/shard_map/all_gather | solution.py:97
  174.7 5.1 %fusion = f32[1,6,64,128]{3,0,2,1:T(1,128)S(1)} fusion(f32[16,6,64,128]{3,2,1,0:T(8,128)} %all-gather.5.cloned.1.call-done, pred[16,16]{1,0:T(8,128)(4,1)S(1)} %fusion.23, s32[]{:T(128)S(6)} %select_n.58, f32[16,16]{1,0:T(8,128)S(1)} %get-tuple-element.65, f32[16,16]{1,0:T(8,128)S(1)} %fusion.27, f32[16,16]{1,0:T(8,128)S(1)} %get-tuple-element.64), kind=kOutput, calls=%fused_computation.10 | convolution fusion | flops 9437376 | bytes 3344388 | tf_op jit(solution)/shard_map/nm,mvbc->nvbc/dot_general | solution.py:94
  179.8 0.6 fusion.7
  180.9 0.7 copy.57
  (52 shorter events, 2.4 us)
Async XLA Ops:
  6.5 49.6 %copy-start.2 = (f32[3,1,6,64,128]{4,3,2,1,0:T(8,128)S(1)}, f32[3,1,6,64,128]{4,3,2,1,0:T(8,128)}, u32[]{:S(2)}) copy-start(f32[3,1,6,64,128]{4,3,2,1,0:T(8,128)} %param.22) | copy-start | bytes 1769476
  6.5 86.1 %all-gather.3.cloned.1.call-start = ((), (), s32[]{:S(2)}) async-start(), calls=%async_computation.6 | async-start | bytes 3342336 | tf_op jit(solution)/shard_map/all_gather | solution.py:97
  8.7 19.0 %all-to-all-start.1 = ((f32[32,1,6,2,128]{4,3,2,1,0:T(2,128)}), f32[32,1,6,2,128]{4,3,2,1,0:T(2,128)S(1)}, u32[]{:S(2)}, u32[]{:S(2)}) async-start(f32[32,1,6,2,128]{4,3,2,1,0:T(2,128)} %broadcast_in_dim.31), calls=%async_computation.1 | async-start | bytes 393216 | tf_op jit(solution)/shard_map/all_to_all | solution.py:14
  27.8 14.1 %all-to-all-start = ((f32[1,6,32,2,128]{4,3,1,0,2:T(2,128)}), f32[1,6,32,2,128]{4,3,1,0,2:T(2,128)S(1)}, u32[]{:S(2)}, u32[]{:S(2)}) async-start(f32[1,6,32,2,128]{4,3,1,0,2:T(2,128)} %bitcast.137), calls=%async_computation | async-start | bytes 393216 | tf_op jit(solution)/shard_map/all_to_all | solution.py:101
  42.5 27.4 %all-to-all-start.2 = ((f32[16,1,6,2,128]{4,3,2,1,0:T(2,128)}), f32[16,1,6,2,128]{4,3,2,1,0:T(2,128)S(1)}, u32[]{:S(2)}, u32[]{:S(2)}) async-start(f32[16,1,6,2,128]{4,3,2,1,0:T(2,128)} %broadcast_in_dim.32), calls=%async_computation.2 | async-start | bytes 196608 | tf_op jit(solution)/shard_map/all_to_all | solution.py:14
  55.8 118.9 %all-gather.5.cloned.1.call-start = ((), (), s32[]{:S(2)}) async-start(), calls=%async_computation.7 | async-start | bytes 3342336 | tf_op jit(solution)/shard_map/all_gather | solution.py:97
  56.0 41.8 %copy-start.1 = (f32[1,6,64,128]{3,2,1,0:T(8,128)S(1)}, f32[1,6,64,128]{3,2,1,0:T(8,128)}, u32[]{:S(2)}) copy-start(f32[1,6,64,128]{3,2,1,0:T(8,128)} %param.21) | copy-start | bytes 589828
  56.3 42.1 %copy-start.3 = (f32[2,128]{1,0:T(2,128)S(1)}, f32[2,128]{1,0:T(2,128)}, u32[]{:S(2)}) copy-start(f32[2,128]{1,0:T(2,128)} %param.28) | copy-start | bytes 3076
  56.9 41.6 %copy-start = (f32[1,6,6,64,128]{4,3,2,1,0:T(8,128)S(1)}, f32[1,6,6,64,128]{4,3,2,1,0:T(8,128)}, u32[]{:S(2)}) copy-start(f32[1,6,6,64,128]{4,3,2,1,0:T(8,128)} %param.23) | copy-start | bytes 3538948
  100.5 13.4 %all-to-all-start.4 = ((f32[32,1,6,2,128]{4,3,2,1,0:T(2,128)}), f32[32,1,6,2,128]{4,3,2,1,0:T(2,128)S(1)}, u32[]{:S(2)}, u32[]{:S(2)}) async-start(f32[32,1,6,2,128]{4,3,2,1,0:T(2,128)} %broadcast_in_dim.35), calls=%async_computation.4 | async-start | bytes 393216 | tf_op jit(solution)/shard_map/all_to_all | solution.py:14
  113.8 12.0 %all-to-all-start.3 = ((f32[1,6,32,2,128]{4,3,1,0,2:T(2,128)}), f32[1,6,32,2,128]{4,3,1,0,2:T(2,128)S(1)}, u32[]{:S(2)}, u32[]{:S(2)}) async-start(f32[1,6,32,2,128]{4,3,1,0,2:T(2,128)} %bitcast.136), calls=%async_computation.3 | async-start | bytes 393216 | tf_op jit(solution)/shard_map/all_to_all | solution.py:101
  126.6 21.9 %all-to-all-start.5 = ((f32[16,1,6,2,128]{4,3,2,1,0:T(2,128)}), f32[16,1,6,2,128]{4,3,2,1,0:T(2,128)S(1)}, u32[]{:S(2)}, u32[]{:S(2)}) async-start(f32[16,1,6,2,128]{4,3,2,1,0:T(2,128)} %broadcast_in_dim.36), calls=%async_computation.5 | async-start | bytes 196608 | tf_op jit(solution)/shard_map/all_to_all | solution.py:14
Sparse Core Ops, SparseCore 0:
  9.4 83.2 all-gather.2
  99.8 74.7 all-gather.4
where the time goes:
time: 189 us; the launch traced here: 188 us
  waiting for transfers between devices  90.6 us (48%)
  starting transfers between devices  49.9 us (26%)
  local copies, waits for them, and re-layouts  17.1 us (9%)
  between operations  13.9 us (7%)
  matrix products  10.2 us (5%)
  other arithmetic  6.78 us (4%)
    all_gather x2, waiting for transfers between devices, per_device(): lax.all_gather(field, 'inst', axis=0, tiled=True)  47.8 us
    all_to_all x4, starting transfers between devices, from_everyone(): lax.all_to_all(jnp.broadcast_to(shard[None], (length, *shard.shape)), axi...  36.9 us
    all_to_all x4, waiting for transfers between devices, from_everyone(): lax.all_to_all(jnp.broadcast_to(shard[None], (length, *shard.shape)), axi...  31.7 us
    all_to_all x2, starting transfers between devices, per_device(): lax.all_to_all(outgoing, 'mesh', split_axis=2, concat_axis=2, tiled=True)  12.9 us
    all_to_all x2, waiting for transfers between devices, per_device(): lax.all_to_all(outgoing, 'mesh', split_axis=2, concat_axis=2, tiled=True)  10.3 us
    dot_general x2, matrix products, per_device(): jnp.einsum('nm,mvbc->nvbc', own_rows, lax.all_gather(field, 'inst', axis=...  10.2 us
  transfers between devices with their start and end apart: 8, of which 7 were waited for; matrix products, arithmetic and copies ran while one was open for 11% of the time, Pallas kernels for 0%

commit v1 on v0

v1 whole, which is shorter than its diff:
```python
import jax
import jax.numpy as jnp
import numpy as np
from jax import lax
from jax.experimental import pallas as pl
from jax.experimental.pallas import tpu as pltpu
from jax.sharding import PartitionSpec as P

NT = 16
NV = 6
CELLS = 128
BLK = 64
NMESH = 32
ROWS = NV * BLK
PIECE = ROWS // NT
SLOT = 4 * NV
BACK = PIECE + 16
SWEEPS = 2
F32 = jnp.float32


def circulant_row():
    k = np.arange(NT, dtype=np.float64)
    parity = 1.0 - 2.0 * (k % 2)
    angle = np.pi * k / NT
    sine = np.where(k == 0, 1.0, np.sin(angle))
    first = np.where(k == 0, 0.0, 0.5 * parity * np.cos(angle) / sine)
    second = np.where(k == 0, -(NT * NT + 2.0) / 12.0, -0.5 * parity / (sine * sine))
    return [float(v) for v in (first - 0.1 * second)]


TABLE = circulant_row()


def pack_blocks(field, send, out):
    faces = [field[pl.ds(b, NV, stride=BLK), :] for b in range(2)]
    for dst in range(NMESH):
        for s in range(2):
            blk = send[s, dst]
            out[pl.ds(dst * SLOT + s * NV, NV), :] = field[pl.ds(blk, NV, stride=BLK), :]
        for b in range(2):
            out[pl.ds(dst * SLOT + (2 + b) * NV, NV), :] = faces[b]


def pack_kernel(field, send, out):
    pack_blocks(field, send, out)


def spectral_kernel(pieces, blocks, donor, weight, out):
    for t in range(PIECE // 8):
        rows = [pieces[pl.ds(m * PIECE + t * 8, 8), :] for m in range(NT)]
        for n in range(NT):
            acc = rows[0] * TABLE[n % NT]
            for m in range(1, NT):
                acc = acc + rows[m] * TABLE[(n - m) % NT]
            out[pl.ds(n * BACK + t * 8, 8), :] = acc
    for j in range(2):
        total = None
        for k in range(2):
            who = donor[j, k]
            row = (who // 2) * SLOT + (2 + who % 2) * NV
            part = blocks[pl.ds(row, NV), :] * weight[j, k]
            total = part if total is None else total + part
        for n in range(NT):
            out[pl.ds(n * BACK + PIECE + j * 8, NV), :] = total


def update_kernel(last, field, right, coup, jac, spec, row_id, recv, coef, shift, inst, blocks, back, *rest):
    if last:
        out, halo, freq = rest
    else:
        send, out, packed, halo, freq = rest
    for b in range(BLK):
        slot = recv[b]
        row = (slot // 2) * SLOT + (slot % 2) * NV
        halo[pl.ds(b, NV, stride=BLK), :] = blocks[pl.ds(row, NV), :]
        freq[pl.ds(b, 1), :] = spec[pl.ds(b, 1), :] * (1.0 + 0.5 * row_id[b].astype(F32))
    lane = lax.broadcasted_iota(jnp.int32, (8, CELLS), 1)
    sub = lax.broadcasted_iota(jnp.int32, (8, CELLS), 0)
    not_first = lane > 0
    not_last = lane < CELLS - 1
    mix_rows = [((inst[0] + shift[j]) % NT) * BACK + PIECE + j * 8 for j in range(2)]
    for t in range(BLK // 8):
        total = []
        f = freq[pl.ds(t * 8, 8), :]
        for v in range(NV):
            r = v * BLK + t * 8
            here = field[pl.ds(r, 8), :]
            below = jnp.where(not_first, pltpu.roll(here, 1, 1), 0.0)
            above = jnp.where(not_last, pltpu.roll(here, CELLS - 1, 1), 0.0)
            p, q = r // PIECE, r % PIECE
            val = right[pl.ds(r, 8), :]
            val = val + (coup[pl.ds(r, 8), :] * below + coup[pl.ds(ROWS + r, 8), :] * above)
            val = val + coup[pl.ds(2 * ROWS + r, 8), :] * halo[pl.ds(r, 8), :]
            val = val - f * back[pl.ds(p * BACK + q, 8), :]
            if t == 0:
                for j in range(2):
                    mix = coef[pl.ds(j, 1), :] * back[pl.ds(mix_rows[j] + v, 1), :]
                    val = jnp.where(sub == j, val + mix, val)
            total.append(val)
        for v in range(NV):
            new = 0.35 * total[v]
            for w in range(NV):
                new = new + jac[pl.ds((v * NV + w) * BLK + t * 8, 8), :] * total[w]
            if v == NV - 1:
                new = jnp.maximum(new, 0.0)
            out[pl.ds(v * BLK + t * 8, 8), :] = new
    if not last:
        pack_blocks(out, send, packed)


def vmem():
    return pl.BlockSpec(memory_space=pltpu.VMEM)


def smem():
    return pl.BlockSpec(memory_space=pltpu.SMEM)


def rows_of(n):
    return jax.ShapeDtypeStruct((n, CELLS), F32)


def swap(x, axis, parts):
    rows = x.shape[0]
    y = lax.all_to_all(x.reshape(parts, rows // parts, CELLS), axis, 0, 0, tiled=True)
    return y.reshape(rows, CELLS)


def per_device(
    state,
    right_side,
    couplings,
    jac_corr,
    spec_scale,
    row_id,
    send_index,
    recv_slot,
    iface_coef,
    donor_index,
    donor_weight,
    phase_shift,
):
    field = state.reshape(ROWS, CELLS)
    right = right_side.reshape(ROWS, CELLS)
    coup = couplings.reshape(3 * ROWS, CELLS)
    jac = jac_corr.reshape(NV * ROWS, CELLS)
    send = send_index.T
    inst = lax.axis_index("inst").astype(jnp.int32).reshape(1)

    packed = pl.pallas_call(
        pack_kernel,
        out_shape=rows_of(NMESH * SLOT),
        in_specs=[vmem(), smem()],
        out_specs=vmem(),
        name="pack",
    )(field, send)
    for sweep in range(SWEEPS):
        last = sweep == SWEEPS - 1
        with jax.named_scope("ahead"):
            pieces = swap(field, "inst", NT)
        with jax.named_scope("blocks"):
            blocks = swap(packed, "mesh", NMESH)
        back = pl.pallas_call(
            spectral_kernel,
            out_shape=rows_of(NT * BACK),
            in_specs=[vmem(), vmem(), smem(), smem()],
            out_specs=vmem(),
            name="spectral",
        )(pieces, blocks, donor_index, donor_weight)
        with jax.named_scope("back"):
            back = swap(back, "inst", NT)
        ins = [field, right, coup, jac, spec_scale, row_id, recv_slot, iface_coef, phase_shift, inst, blocks, back]
        specs = [vmem(), vmem(), vmem(), vmem(), vmem(), smem(), smem(), vmem(), smem(), smem(), vmem(), vmem()]
        shapes = [rows_of(ROWS)]
        if not last:
            ins.append(send)
            specs.append(smem())
            shapes.append(rows_of(NMESH * SLOT))
        res = pl.pallas_call(
            lambda *refs, last=last: update_kernel(last, *refs),
            out_shape=shapes,
            in_specs=specs,
            out_specs=[vmem()] * len(shapes),
            scratch_shapes=[pltpu.VMEM((ROWS, CELLS), F32), pltpu.VMEM((BLK, CELLS), F32)],
            name="update",
        )(*ins)
        field = res[0]
        if not last:
            packed = res[1]
    return field.reshape(1, NV, BLK, CELLS)


def solution(mesh):
    return jax.shard_map(
        per_device,
        mesh=mesh,
        in_specs=(
            P("inst", None, "mesh", None),
            P("inst", None, "mesh", None),
            P(None, "inst", None, "mesh", None),
            P("inst", None, None, "mesh", None),
            P("mesh", None),
            P("mesh"),
            P("mesh", None),
            P("mesh"),
            P("mesh", None),
            P("mesh", None),
            P("mesh", None),
            P("mesh"),
        ),
        out_specs=P("inst", None, "mesh", None),
        check_vma=False,
    )
```

time: 189 us -> 153 us (0.81)
  blocking collectives: 0 us -> 111 us
  waiting for transfers between devices: 90.6 us -> 21.3 us
  starting transfers between devices: 49.9 us -> 6.23 us
  local copies, waits for them, and re-layouts: 17.1 us -> 0.73 us
  between operations: 13.9 us -> 0.02 us
  Pallas kernels: 0 us -> 12.6 us
  matrix products: 10.2 us -> 0 us
  other arithmetic: 6.78 us -> 0 us
    all_to_all x0 -> x5, blocking collectives: none -> 111 us  [swap(): lax.all_to_all(x.reshape(parts, rows // parts, CELLS), axis, 0, 0, tiled=...]
    all_gather x2 -> x0, waiting for transfers between devices: 47.8 us -> none  [per_device(): lax.all_gather(field, 'inst', axis=0, tiled=True)]
    all_to_all x6 -> x1, starting transfers between devices: 49.9 us -> 6.23 us  [swap(): lax.all_to_all(x.reshape(parts, rows // parts, CELLS), axis, 0, 0, tiled=...]
    all_to_all x6 -> x1, waiting for transfers between devices: 42.1 us -> 21.3 us  [swap(): lax.all_to_all(x.reshape(parts, rows // parts, CELLS), axis, 0, 0, tiled=...]
    pallas_call x0 -> x5, Pallas kernels: none -> 12.6 us  [the longest x2 6.51 us: per_device(): pl.pallas_call(lambda *refs, last=last: update_kernel(last, *refs), out_s...]
    dot_general x2 -> x0, matrix products: 10.2 us -> none  [per_device(): jnp.einsum('nm,mvbc->nvbc', own_rows, lax.all_gather(field, 'inst', axis=...]
    gather x12 -> x0, local copies, waits for them, and re-layouts: 7.38 us -> none  [the longest x4 2.82 us: per_device(): outgoing = field[:, :, send_index]]
    broadcast_in_dim x8 -> x0, local copies, waits for them, and re-layouts: 3.65 us -> none  [the longest x7 3.55 us: from_everyone(): jnp.broadcast_to(shard[None], (length, *shard.shape))]
  transfers between devices with their start and end apart: 8 -> 1, of which waited for: 7 -> 1; matrix products, arithmetic and copies ran while one was open for 11% -> 0% of each run, Pallas kernels for 0% -> 0%
where the time goes in v1:
time: 153 us; the launch traced here: 152 us
  blocking collectives  111 us (73%)
  waiting for transfers between devices  21.3 us (14%)
  Pallas kernels  12.6 us (8%)
  starting transfers between devices  6.23 us (4%)
    all_to_all x5, blocking collectives, swap(): lax.all_to_all(x.reshape(parts, rows // parts, CELLS), axis, 0, 0, tiled=...  111 us
    all_to_all x1, waiting for transfers between devices, swap(): lax.all_to_all(x.reshape(parts, rows // parts, CELLS), axis, 0, 0, tiled=...  21.3 us
    pallas_call x2, Pallas kernels, per_device(): pl.pallas_call(lambda *refs, last=last: update_kernel(last, *refs), out_s...  6.51 us
    all_to_all x1, starting transfers between devices, swap(): lax.all_to_all(x.reshape(parts, rows // parts, CELLS), axis, 0, 0, tiled=...  6.23 us
    pallas_call x2, Pallas kernels, per_device(): pl.pallas_call(spectral_kernel, out_shape=rows_of(NT * BACK), in_specs=[v...  4.11 us
  transfers between devices with their start and end apart: 1, of which 1 were waited for; matrix products, arithmetic and copies ran while one was open for 0% of the time, Pallas kernels for 0%

profile of v1, /device:TPU:6, one launch (start us, length us, event | category | flops | bytes accessed | tf_op | source)
XLA Modules:
  0.0 151.5 jit_solution(17028900683165967257)
XLA Ops:
  0.0 0.0 copy-start
  0.0 2.0 %pack.1 = f32[768,128]{1,0:T(8,128)} custom-call(f32[384,128]{1,0:T(8,128)} %bitcast.27, s32[2,32]{1,0:T(2,128)} %bitcast.41), custom_call_target="tpu_custom_call" | custom-call | tf_op jit(solution)/shard_map/pack/pallas_call | solution.py:151
  2.0 18.2 %all_to_all.30 = f32[32,24,128]{2,1,0:T(8,128)} all-to-all(f32[32,24,128]{2,1,0:T(8,128)} %bitcast.30), channel_id=1, replica_groups=mesh['inst'=16,'mesh'=32] {'mesh'}, dimensions={0} | all-to-all | bytes 786432 | tf_op jit(solution)/shard_map/blocks/all_to_all | solution.py:126
  20.2 0.0 copy-done
  20.2 28.8 %all_to_all.31 = f32[16,24,128]{2,1,0:T(8,128)} all-to-all(f32[16,24,128]{2,1,0:T(8,128)S(1)} %bitcast.29), channel_id=1, replica_groups=mesh['inst'=16,'mesh'=32] {'inst'}, dimensions={0} | all-to-all | bytes 393216 | tf_op jit(solution)/shard_map/ahead/all_to_all | solution.py:126
  49.0 2.1 %spectral.2 = f32[640,128]{1,0:T(8,128)} custom-call(f32[384,128]{1,0:T(8,128)} %bitcast.38, f32[768,128]{1,0:T(8,128)} %bitcast.23, s32[2,2]{1,0:T(2,128)} %donor.3, f32[2,2]{1,0:T(2,128)} %weight.3), custom_call_target="tpu_custom_call" | custom-call | tf_op jit(solution)/shard_map/spectral/pallas_call | solution.py:164
  51.1 6.2 %all-to-all-start.2 = ((f32[16,40,128]{2,1,0:T(8,128)}), f32[16,40,128]{2,1,0:T(8,128)S(1)}, u32[]{:S(2)}, u32[]{:S(2)}) async-start(f32[16,40,128]{2,1,0:T(8,128)} %bitcast.31), calls=%async_computation.2 | async-start | bytes 655360 | tf_op jit(solution)/shard_map/back/all_to_all | solution.py:126
  57.3 21.3 %all-to-all-done.2 = f32[16,40,128]{2,1,0:T(8,128)S(1)} async-done(((f32[16,40,128]{2,1,0:T(8,128)}), f32[16,40,128]{2,1,0:T(8,128)S(1)}, u32[]{:S(2)}, u32[]{:S(2)}) %all-to-all-start.2) | async-done | bytes 327712 | tf_op jit(solution)/shard_map/back/all_to_all | solution.py:126
  78.6 0.0 copy-start.1
  78.6 0.7 copy-done.1
  79.3 3.4 %update.2 = (f32[384,128]{1,0:T(8,128)}, f32[768,128]{1,0:T(8,128)}) custom-call(f32[384,128]{1,0:T(8,128)} %bitcast.28, f32[384,128]{1,0:T(8,128)} %bitcast.35, f32[1152,128]{1,0:T(8,128)} %bitcast.25, f32[2304,128]{1,0:T(8,128)} %bitcast.19, f32[64,128]{1,0:T(8,128)} %refs_4_.3, s32[64]{0:T(128)} %refs_5_.3, s32[64]{0:T(128)} %refs_6_.3, ...), custom_call_target="tpu_custom_call" | custom-call | tf_op jit(solution)/shard_map/update/pallas_call | solution.py:180
  82.7 13.7 %all_to_all.32 = f32[32,24,128]{2,1,0:T(8,128)} all-to-all(f32[32,24,128]{2,1,0:T(8,128)} %bitcast.40), channel_id=1, replica_groups=mesh['inst'=16,'mesh'=32] {'mesh'}, dimensions={0} | all-to-all | bytes 786432 | tf_op jit(solution)/shard_map/blocks/all_to_all | solution.py:126
  96.4 22.4 %all_to_all.33 = f32[16,24,128]{2,1,0:T(8,128)} all-to-all(f32[16,24,128]{2,1,0:T(8,128)} %bitcast.37), channel_id=1, replica_groups=mesh['inst'=16,'mesh'=32] {'inst'}, dimensions={0} | all-to-all | bytes 393216 | tf_op jit(solution)/shard_map/ahead/all_to_all | solution.py:126
  118.8 2.0 %spectral.3 = f32[640,128]{1,0:T(8,128)} custom-call(f32[384,128]{1,0:T(8,128)} %bitcast.39, f32[768,128]{1,0:T(8,128)} %bitcast.21, s32[2,2]{1,0:T(2,128)} %donor.3, f32[2,2]{1,0:T(2,128)} %weight.3), custom_call_target="tpu_custom_call" | custom-call | tf_op jit(solution)/shard_map/spectral/pallas_call | solution.py:164
  120.8 27.6 %all_to_all.34 = f32[16,40,128]{2,1,0:T(8,128)} all-to-all(f32[16,40,128]{2,1,0:T(8,128)} %bitcast.33), channel_id=1, replica_groups=mesh['inst'=16,'mesh'=32] {'inst'}, dimensions={0} | all-to-all | bytes 655360 | tf_op jit(solution)/shard_map/back/all_to_all | solution.py:126
  148.4 3.1 %update.3 = f32[384,128]{1,0:T(8,128)} custom-call(f32[384,128]{1,0:T(8,128)} %get-tuple-element.7.refs_0_, f32[384,128]{1,0:T(8,128)} %bitcast.36, f32[1152,128]{1,0:T(8,128)} %bitcast.26, f32[2304,128]{1,0:T(8,128)} %bitcast.20, f32[64,128]{1,0:T(8,128)} %refs_4_.3, s32[64]{0:T(128)} %refs_5_.3, s32[64]{0:T(128)} %refs_6_.3, f32[2,128]{1,0:T(2,128)} %refs_7_.3, ...), custom_call_target="tpu_custom_call" | custom-call | tf_op jit(solution)/shard_map/update/pallas_call | solution.py:180
Async XLA Ops:
  0.0 20.2 %copy-start = (f32[1,6,64,128]{3,2,1,0:T(8,128)S(1)}, f32[1,6,64,128]{3,2,1,0:T(8,128)}, u32[]{:S(2)}) copy-start(f32[1,6,64,128]{3,2,1,0:T(8,128)} %param.12) | copy-start | bytes 589828
  51.1 27.5 %all-to-all-start.2 = ((f32[16,40,128]{2,1,0:T(8,128)}), f32[16,40,128]{2,1,0:T(8,128)S(1)}, u32[]{:S(2)}, u32[]{:S(2)}) async-start(f32[16,40,128]{2,1,0:T(8,128)} %bitcast.31), calls=%async_computation.2 | async-start | bytes 655360 | tf_op jit(solution)/shard_map/back/all_to_all | solution.py:126
  78.6 0.7 copy-start.1

commit v2 on v1

--- a/solution.py
+++ b/solution.py
@@ -14,7 +14,7 @@
 ROWS = NV * BLK
 PIECE = ROWS // NT
 SLOT = 4 * NV
-BACK = PIECE + 16
+LEG = PIECE + 1
 SWEEPS = 2
 F32 = jnp.float32
 
@@ -46,14 +46,9 @@
     pack_blocks(field, send, out)
 
 
-def spectral_kernel(pieces, blocks, donor, weight, out):
-    for t in range(PIECE // 8):
-        rows = [pieces[pl.ds(m * PIECE + t * 8, 8), :] for m in range(NT)]
-        for n in range(NT):
-            acc = rows[0] * TABLE[n % NT]
-            for m in range(1, NT):
-                acc = acc + rows[m] * TABLE[(n - m) % NT]
-            out[pl.ds(n * BACK + t * 8, 8), :] = acc
+def mix_kernel(field, blocks, donor, weight, out):
+    for p in range(NT):
+        out[pl.ds(p * LEG, PIECE), :] = field[pl.ds(p * PIECE, PIECE), :]
     for j in range(2):
         total = None
         for k in range(2):
@@ -61,11 +56,27 @@
             row = (who // 2) * SLOT + (2 + who % 2) * NV
             part = blocks[pl.ds(row, NV), :] * weight[j, k]
             total = part if total is None else total + part
+        for v in range(NV):
+            out[pl.ds((j * NV + v) * LEG + PIECE, 1), :] = total[v : v + 1]
+    for p in range(2 * NV, NT):
+        out[pl.ds(p * LEG + PIECE, 1), :] = jnp.zeros((1, CELLS), F32)
+
+
+def spectral_kernel(legs, shift, inst, out):
+    for t in range(PIECE // 8):
+        rows = [legs[pl.ds(m * LEG + t * 8, 8), :] for m in range(NT)]
         for n in range(NT):
-            out[pl.ds(n * BACK + PIECE + j * 8, NV), :] = total
-
-
-def update_kernel(last, field, right, coup, jac, spec, row_id, recv, coef, shift, inst, blocks, back, *rest):
+            acc = rows[0] * TABLE[n % NT]
+            for m in range(1, NT):
+                acc = acc + rows[m] * TABLE[(n - m) % NT]
+            out[pl.ds(n * LEG + t * 8, 8), :] = acc
+    turn = jnp.where(inst[0] < NV, shift[0], shift[1])
+    for n in range(NT):
+        src = ((n + turn) % NT) * LEG + PIECE
+        out[pl.ds(n * LEG + PIECE, 1), :] = legs[pl.ds(src, 1), :]
+
+
+def update_kernel(last, field, right, coup, jac, spec, row_id, recv, coef, blocks, back, *rest):
     if last:
         out, halo, freq = rest
     else:
@@ -79,7 +90,6 @@
     sub = lax.broadcasted_iota(jnp.int32, (8, CELLS), 0)
     not_first = lane > 0
     not_last = lane < CELLS - 1
-    mix_rows = [((inst[0] + shift[j]) % NT) * BACK + PIECE + j * 8 for j in range(2)]
     for t in range(BLK // 8):
         total = []
         f = freq[pl.ds(t * 8, 8), :]
@@ -92,10 +102,10 @@
             val = right[pl.ds(r, 8), :]
             val = val + (coup[pl.ds(r, 8), :] * below + coup[pl.ds(ROWS + r, 8), :] * above)
             val = val + coup[pl.ds(2 * ROWS + r, 8), :] * halo[pl.ds(r, 8), :]
-            val = val - f * back[pl.ds(p * BACK + q, 8), :]
+            val = val - f * back[pl.ds(p * LEG + q, 8), :]
             if t == 0:
                 for j in range(2):
-                    mix = coef[pl.ds(j, 1), :] * back[pl.ds(mix_rows[j] + v, 1), :]
+                    mix = coef[pl.ds(j, 1), :] * back[pl.ds((j * NV + v) * LEG + PIECE, 1), :]
                     val = jnp.where(sub == j, val + mix, val)
             total.append(val)
         for v in range(NV):
@@ -125,6 +135,11 @@
     rows = x.shape[0]
     y = lax.all_to_all(x.reshape(parts, rows // parts, CELLS), axis, 0, 0, tiled=True)
     return y.reshape(rows, CELLS)
+
+
+def swap_rows(x):
+    y = lax.all_to_all(x.reshape(NT, LEG, 1, CELLS), "inst", 0, 0, tiled=True)
+    return y.reshape(NT * LEG, CELLS)
 
 
 def per_device(
@@ -157,21 +172,25 @@
     )(field, send)
     for sweep in range(SWEEPS):
         last = sweep == SWEEPS - 1
-        with jax.named_scope("ahead"):
-            pieces = swap(field, "inst", NT)
-        with jax.named_scope("blocks"):
-            blocks = swap(packed, "mesh", NMESH)
+        blocks = swap(packed, "mesh", NMESH)
+        legs = pl.pallas_call(
+            mix_kernel,
+            out_shape=rows_of(NT * LEG),
+            in_specs=[vmem(), vmem(), smem(), smem()],
+            out_specs=vmem(),
+            name="mix",
+        )(field, blocks, donor_index, donor_weight)
+        legs = swap_rows(legs)
         back = pl.pallas_call(
             spectral_kernel,
-            out_shape=rows_of(NT * BACK),
-            in_specs=[vmem(), vmem(), smem(), smem()],
+            out_shape=rows_of(NT * LEG),
+            in_specs=[vmem(), smem(), smem()],
             out_specs=vmem(),
             name="spectral",
-        )(pieces, blocks, donor_index, donor_weight)
-        with jax.named_scope("back"):
-            back = swap(back, "inst", NT)
-        ins = [field, right, coup, jac, spec_scale, row_id, recv_slot, iface_coef, phase_shift, inst, blocks, back]
-        specs = [vmem(), vmem(), vmem(), vmem(), vmem(), smem(), smem(), vmem(), smem(), smem(), vmem(), vmem()]
+        )(legs, phase_shift, inst)
+        back = swap_rows(back)
+        ins = [field, right, coup, jac, spec_scale, row_id, recv_slot, iface_coef, blocks, back]
+        specs = [vmem(), vmem(), vmem(), vmem(), vmem(), smem(), smem(), vmem(), vmem(), vmem()]
         shapes = [rows_of(ROWS)]
         if not last:
             ins.append(send)

time: 153 us -> 147 us (0.961)
  blocking collectives: 111 us -> 99.4 us
  starting transfers between devices: 6.23 us -> 12.7 us
  waiting for transfers between devices: 21.3 us -> 16.6 us
  Pallas kernels: 12.6 us -> 15.6 us
    all_to_all x5 -> x2, blocking collectives: 111 us -> 32.7 us  [swap(): lax.all_to_all(x.reshape(parts, rows // parts, CELLS), axis, 0, 0, tiled=...]
    all_to_all x0 -> x3, blocking collectives: none -> 66.8 us  [swap_rows(): y = lax.all_to_all(x.reshape(NT, LEG, 1, CELLS), 'inst', 0, 0, tiled=True)]
    all_to_all x1, starting transfers between devices: 6.23 us -> 12.7 us  [swap_rows(): y = lax.all_to_all(x.reshape(NT, LEG, 1, CELLS), 'inst', 0, 0, tiled=True)]
    all_to_all x1, waiting for transfers between devices: 21.3 us -> 16.6 us  [swap_rows(): y = lax.all_to_all(x.reshape(NT, LEG, 1, CELLS), 'inst', 0, 0, tiled=True)]
    pallas_call x2 -> x4, Pallas kernels: 4.11 us -> 7.3 us  [the longest x2 3.65 us: per_device(): pl.pallas_call(spectral_kernel, out_shape=rows_of(NT * LEG), in_specs=[vm...]
where the time goes in v2:
time: 147 us; the launch traced here: 145 us
  blocking collectives  99.4 us (68%)
  waiting for transfers between devices  16.6 us (11%)
  Pallas kernels  15.6 us (11%)
  starting transfers between devices  12.7 us (9%)
    all_to_all x3, blocking collectives, swap_rows(): y = lax.all_to_all(x.reshape(NT, LEG, 1, CELLS), 'inst', 0, 0, tiled=True)  66.8 us
    all_to_all x2, blocking collectives, swap(): lax.all_to_all(x.reshape(parts, rows // parts, CELLS), axis, 0, 0, tiled=...  32.7 us
    all_to_all x1, waiting for transfers between devices, swap_rows(): y = lax.all_to_all(x.reshape(NT, LEG, 1, CELLS), 'inst', 0, 0, tiled=True)  16.6 us
    all_to_all x1, starting transfers between devices, swap_rows(): y = lax.all_to_all(x.reshape(NT, LEG, 1, CELLS), 'inst', 0, 0, tiled=True)  12.7 us
    pallas_call x2, Pallas kernels, per_device(): pl.pallas_call(lambda *refs, last=last: update_kernel(last, *refs), out_s...  6.38 us
    pallas_call x2, Pallas kernels, per_device(): pl.pallas_call(spectral_kernel, out_shape=rows_of(NT * LEG), in_specs=[vm...  3.65 us
    pallas_call x2, Pallas kernels, per_device(): pl.pallas_call(mix_kernel, out_shape=rows_of(NT * LEG), in_specs=[vmem(),...  3.65 us
  transfers between devices with their start and end apart: 1, of which 1 were waited for; matrix products, arithmetic and copies ran while one was open for 0% of the time, Pallas kernels for 0%

profile of v2, /device:TPU:6, one launch (start us, length us, event | category | flops | bytes accessed | tf_op | source)
XLA Modules:
  0.0 145.0 jit_solution(925968225714944474)
XLA Ops:
  0.0 1.9 %pack.1 = f32[768,128]{1,0:T(8,128)} custom-call(f32[384,128]{1,0:T(8,128)} %bitcast.27, s32[2,32]{1,0:T(2,128)} %bitcast.42), custom_call_target="tpu_custom_call" | custom-call | tf_op jit(solution)/shard_map/pack/pallas_call | solution.py:166
  1.9 18.2 %all_to_all.30 = f32[32,24,128]{2,1,0:T(8,128)} all-to-all(f32[32,24,128]{2,1,0:T(8,128)} %bitcast.30), channel_id=1, replica_groups=mesh['inst'=16,'mesh'=32] {'mesh'}, dimensions={0} | all-to-all | bytes 786432 | tf_op jit(solution)/shard_map/all_to_all | solution.py:136
  20.1 1.8 %mix.2 = f32[400,128]{1,0:T(8,128)} custom-call(f32[384,128]{1,0:T(8,128)} %bitcast.28, f32[768,128]{1,0:T(8,128)} %bitcast.23, s32[2,2]{1,0:T(2,128)} %donor.3, f32[2,2]{1,0:T(2,128)} %weight.3), custom_call_target="tpu_custom_call" | custom-call | tf_op jit(solution)/shard_map/mix/pallas_call | solution.py:176
  21.9 12.7 %all-to-all-start.1 = ((f32[16,25,1,128]{3,2,1,0:T(1,128)}), f32[16,25,1,128]{3,2,1,0:T(1,128)S(1)}, u32[]{:S(2)}, u32[]{:S(2)}) async-start(f32[16,25,1,128]{3,2,1,0:T(1,128)} %bitcast.34), calls=%async_computation.1 | async-start | bytes 409600 | tf_op jit(solution)/shard_map/all_to_all | solution.py:141
  34.6 16.6 %all-to-all-done.1 = f32[16,25,1,128]{3,2,1,0:T(1,128)S(1)} async-done(((f32[16,25,1,128]{3,2,1,0:T(1,128)}), f32[16,25,1,128]{3,2,1,0:T(1,128)S(1)}, u32[]{:S(2)}, u32[]{:S(2)}) %all-to-all-start.1) | async-done | bytes 204832 | tf_op jit(solution)/shard_map/all_to_all | solution.py:141
  51.2 0.0 copy-start
  51.2 0.7 copy-done
  51.9 1.8 %spectral.2 = f32[400,128]{1,0:T(8,128)} custom-call(f32[400,128]{1,0:T(8,128)} %bitcast.33, s32[2]{0:T(128)} %shift.3, s32[1]{0:T(128)} %bitcast.9.inst), custom_call_target="tpu_custom_call" | custom-call | tf_op jit(solution)/shard_map/spectral/pallas_call | solution.py:184
  53.7 22.5 %all_to_all.31 = f32[16,25,1,128]{3,2,1,0:T(1,128)} all-to-all(f32[16,25,1,128]{3,2,1,0:T(1,128)} %bitcast.37), channel_id=1, replica_groups=mesh['inst'=16,'mesh'=32] {'inst'}, dimensions={0} | all-to-all | bytes 409600 | tf_op jit(solution)/shard_map/all_to_all | solution.py:141
  76.2 3.3 %update.2 = (f32[384,128]{1,0:T(8,128)}, f32[768,128]{1,0:T(8,128)}) custom-call(f32[384,128]{1,0:T(8,128)} %bitcast.29, f32[384,128]{1,0:T(8,128)} %bitcast.39, f32[1152,128]{1,0:T(8,128)} %bitcast.25, f32[2304,128]{1,0:T(8,128)} %bitcast.19, f32[64,128]{1,0:T(8,128)} %refs_4_.3, s32[64]{0:T(128)} %refs_5_.3, s32[64]{0:T(128)} %refs_6_.3, ...), custom_call_target="tpu_custom_call" | custom-call | tf_op jit(solution)/shard_map/update/pallas_call | solution.py:199
  79.6 14.5 %all_to_all.32 = f32[32,24,128]{2,1,0:T(8,128)} all-to-all(f32[32,24,128]{2,1,0:T(8,128)} %bitcast.41), channel_id=1, replica_groups=mesh['inst'=16,'mesh'=32] {'mesh'}, dimensions={0} | all-to-all | bytes 786432 | tf_op jit(solution)/shard_map/all_to_all | solution.py:136
  94.0 1.8 %mix.3 = f32[400,128]{1,0:T(8,128)} custom-call(f32[384,128]{1,0:T(8,128)} %get-tuple-element.7.field.refs_0_, f32[768,128]{1,0:T(8,128)} %bitcast.21, s32[2,2]{1,0:T(2,128)} %donor.3, f32[2,2]{1,0:T(2,128)} %weight.3), custom_call_target="tpu_custom_call" | custom-call | tf_op jit(solution)/shard_map/mix/pallas_call | solution.py:176
  95.8 21.8 %all_to_all.33 = f32[16,25,1,128]{3,2,1,0:T(1,128)} all-to-all(f32[16,25,1,128]{3,2,1,0:T(1,128)} %bitcast.38), channel_id=1, replica_groups=mesh['inst'=16,'mesh'=32] {'inst'}, dimensions={0} | all-to-all | bytes 409600 | tf_op jit(solution)/shard_map/all_to_all | solution.py:141
  117.7 1.8 %spectral.3 = f32[400,128]{1,0:T(8,128)} custom-call(f32[400,128]{1,0:T(8,128)} %bitcast.35, s32[2]{0:T(128)} %shift.3, s32[1]{0:T(128)} %bitcast.9.inst), custom_call_target="tpu_custom_call" | custom-call | tf_op jit(solution)/shard_map/spectral/pallas_call | solution.py:184
  119.5 22.5 %all_to_all.34 = f32[16,25,1,128]{3,2,1,0:T(1,128)} all-to-all(f32[16,25,1,128]{3,2,1,0:T(1,128)} %bitcast.36), channel_id=1, replica_groups=mesh['inst'=16,'mesh'=32] {'inst'}, dimensions={0} | all-to-all | bytes 409600 | tf_op jit(solution)/shard_map/all_to_all | solution.py:141
  142.0 3.0 %update.3 = f32[384,128]{1,0:T(8,128)} custom-call(f32[384,128]{1,0:T(8,128)} %get-tuple-element.7.field.refs_0_, f32[384,128]{1,0:T(8,128)} %bitcast.40, f32[1152,128]{1,0:T(8,128)} %bitcast.26, f32[2304,128]{1,0:T(8,128)} %bitcast.20, f32[64,128]{1,0:T(8,128)} %refs_4_.3, s32[64]{0:T(128)} %refs_5_.3, s32[64]{0:T(128)} %refs_6_.3, f32[2,128]{1,0:T(2,128)} %refs_7_.3, ...), custom_call_target="tpu_custom_call" | custom-call | tf_op jit(solution)/shard_map/update/pallas_call | solution.py:199
Async XLA Ops:
  21.9 29.3 %all-to-all-start.1 = ((f32[16,25,1,128]{3,2,1,0:T(1,128)}), f32[16,25,1,128]{3,2,1,0:T(1,128)S(1)}, u32[]{:S(2)}, u32[]{:S(2)}) async-start(f32[16,25,1,128]{3,2,1,0:T(1,128)} %bitcast.34), calls=%async_computation.1 | async-start | bytes 409600 | tf_op jit(solution)/shard_map/all_to_all | solution.py:141
  51.2 0.7 copy-start

commit v3 on v2

--- a/solution.py
+++ b/solution.py
@@ -42,13 +42,15 @@
             out[pl.ds(dst * SLOT + (2 + b) * NV, NV), :] = faces[b]
 
 
-def pack_kernel(field, send, out):
+def pack_kernel(field, send, out, legs):
     pack_blocks(field, send, out)
-
-
-def mix_kernel(field, blocks, donor, weight, out):
     for p in range(NT):
-        out[pl.ds(p * LEG, PIECE), :] = field[pl.ds(p * PIECE, PIECE), :]
+        legs[pl.ds(p * LEG, PIECE), :] = field[pl.ds(p * PIECE, PIECE), :]
+        legs[pl.ds(p * LEG + PIECE, 1), :] = jnp.zeros((1, CELLS), F32)
+
+
+def mix_kernel(legs, blocks, donor, weight, out):
+    out[...] = legs[...]
     for j in range(2):
         total = None
         for k in range(2):
@@ -58,8 +60,6 @@
             total = part if total is None else total + part
         for v in range(NV):
             out[pl.ds((j * NV + v) * LEG + PIECE, 1), :] = total[v : v + 1]
-    for p in range(2 * NV, NT):
-        out[pl.ds(p * LEG + PIECE, 1), :] = jnp.zeros((1, CELLS), F32)
 
 
 def spectral_kernel(legs, shift, inst, out):
@@ -71,16 +71,15 @@
                 acc = acc + rows[m] * TABLE[(n - m) % NT]
             out[pl.ds(n * LEG + t * 8, 8), :] = acc
     turn = jnp.where(inst[0] < NV, shift[0], shift[1])
-    for n in range(NT):
-        src = ((n + turn) % NT) * LEG + PIECE
-        out[pl.ds(n * LEG + PIECE, 1), :] = legs[pl.ds(src, 1), :]
+    mixes = legs[pl.ds(PIECE, NT, stride=LEG), :]
+    out[pl.ds(PIECE, NT, stride=LEG), :] = pltpu.roll(mixes, NT - turn, 0)
 
 
 def update_kernel(last, field, right, coup, jac, spec, row_id, recv, coef, blocks, back, *rest):
     if last:
         out, halo, freq = rest
     else:
-        send, out, packed, halo, freq = rest
+        send, out, packed, legs, halo, freq = rest
     for b in range(BLK):
         slot = recv[b]
         row = (slot // 2) * SLOT + (slot % 2) * NV
@@ -114,7 +113,10 @@
                 new = new + jac[pl.ds((v * NV + w) * BLK + t * 8, 8), :] * total[w]
             if v == NV - 1:
                 new = jnp.maximum(new, 0.0)
-            out[pl.ds(v * BLK + t * 8, 8), :] = new
+            r = v * BLK + t * 8
+            out[pl.ds(r, 8), :] = new
+            if not last:
+                legs[pl.ds((r // PIECE) * LEG + r % PIECE, 8), :] = new
     if not last:
         pack_blocks(out, send, packed)
 
@@ -156,57 +158,74 @@
     donor_weight,
     phase_shift,
 ):
+    near = lambda x: pltpu.with_memory_space_constraint(x, pltpu.VMEM)
+    small = lambda x: x
     field = state.reshape(ROWS, CELLS)
-    right = right_side.reshape(ROWS, CELLS)
-    coup = couplings.reshape(3 * ROWS, CELLS)
-    jac = jac_corr.reshape(NV * ROWS, CELLS)
-    send = send_index.T
-    inst = lax.axis_index("inst").astype(jnp.int32).reshape(1)
-
-    packed = pl.pallas_call(
+    right = near(right_side.reshape(ROWS, CELLS))
+    coup = near(couplings.reshape(3 * ROWS, CELLS))
+    jac = near(jac_corr.reshape(NV * ROWS, CELLS))
+    spec = near(spec_scale)
+    send = small(send_index.T)
+    inst = small(lax.axis_index("inst").astype(jnp.int32).reshape(1))
+    donor = small(donor_index)
+    weight = small(donor_weight)
+    shift = small(phase_shift)
+    recv = small(recv_slot)
+    blade = small(row_id)
+
+    packed, legs = pl.pallas_call(
         pack_kernel,
-        out_shape=rows_of(NMESH * SLOT),
+        out_shape=[rows_of(NMESH * SLOT), rows_of(NT * LEG)],
         in_specs=[vmem(), smem()],
-        out_specs=vmem(),
+        out_specs=[vmem()] * 2,
         name="pack",
-    )(field, send)
+        compiler_params=pltpu.CompilerParams(vmem_limit_bytes=8 << 20),
+    )(near(field), send)
     for sweep in range(SWEEPS):
         last = sweep == SWEEPS - 1
-        blocks = swap(packed, "mesh", NMESH)
+        blocks = near(swap(packed, "mesh", NMESH))
         legs = pl.pallas_call(
             mix_kernel,
             out_shape=rows_of(NT * LEG),
             in_specs=[vmem(), vmem(), smem(), smem()],
             out_specs=vmem(),
+            input_output_aliases={0: 0},
             name="mix",
-        )(field, blocks, donor_index, donor_weight)
-        legs = swap_rows(legs)
+            compiler_params=pltpu.CompilerParams(vmem_limit_bytes=8 << 20),
+        )(near(legs), blocks, donor, weight)
+        legs = near(swap_rows(legs))
         back = pl.pallas_call(
             spectral_kernel,
             out_shape=rows_of(NT * LEG),
             in_specs=[vmem(), smem(), smem()],
             out_specs=vmem(),
+            input_output_aliases={0: 0},
             name="spectral",
-        )(legs, phase_shift, inst)
-        back = swap_rows(back)
-        ins = [field, right, coup, jac, spec_scale, row_id, recv_slot, iface_coef, blocks, back]
+            compiler_params=pltpu.CompilerParams(vmem_limit_bytes=8 << 20),
+        )(legs, shift, inst)
+        back = near(swap_rows(back))
+        ins = [near(field), right, coup, jac, spec, blade, recv, iface_coef, blocks, back]
         specs = [vmem(), vmem(), vmem(), vmem(), vmem(), smem(), smem(), vmem(), vmem(), vmem()]
         shapes = [rows_of(ROWS)]
+        alias = {}
         if not last:
             ins.append(send)
             specs.append(smem())
-            shapes.append(rows_of(NMESH * SLOT))
+            shapes += [rows_of(NMESH * SLOT), rows_of(NT * LEG)]
+            alias = {0: 0, 8: 1, 9: 2}
         res = pl.pallas_call(
             lambda *refs, last=last: update_kernel(last, *refs),
             out_shape=shapes,
             in_specs=specs,
             out_specs=[vmem()] * len(shapes),
             scratch_shapes=[pltpu.VMEM((ROWS, CELLS), F32), pltpu.VMEM((BLK, CELLS), F32)],
+            input_output_aliases=alias,
             name="update",
+            compiler_params=pltpu.CompilerParams(vmem_limit_bytes=8 << 20),
         )(*ins)
         field = res[0]
         if not last:
-            packed = res[1]
+            packed, legs = res[1], res[2]
     return field.reshape(1, NV, BLK, CELLS)
 
 

time: 147 us -> 139 us (0.946)
  Pallas kernels: 15.6 us -> 8.62 us
  blocking collectives: 99.4 us -> 96.2 us
    pallas_call x2, Pallas kernels: 6.38 us -> 3.26 us  [per_device(): pl.pallas_call(lambda *refs, last=last: update_kernel(last, *refs), out_s...]
    all_to_all x2, blocking collectives: 32.7 us -> 29.8 us  [swap(): lax.all_to_all(x.reshape(parts, rows // parts, CELLS), axis, 0, 0, tiled=...]
    pallas_call x2, Pallas kernels: 3.65 us -> 1.51 us  [per_device(): pl.pallas_call(spectral_kernel, out_shape=rows_of(NT * LEG), in_specs=[vm...]
where the time goes in v3:
time: 139 us; the launch traced here: 137 us
  blocking collectives  96.2 us (69%)
  waiting for transfers between devices  16.6 us (12%)
  starting transfers between devices  14 us (10%)
  Pallas kernels  8.62 us (6%)
  local copies, waits for them, and re-layouts  1.7 us (1%)
    all_to_all x3, blocking collectives, swap_rows(): y = lax.all_to_all(x.reshape(NT, LEG, 1, CELLS), 'inst', 0, 0, tiled=True)  66.5 us
    all_to_all x2, blocking collectives, swap(): lax.all_to_all(x.reshape(parts, rows // parts, CELLS), axis, 0, 0, tiled=...  29.8 us
    all_to_all x1, waiting for transfers between devices, swap_rows(): y = lax.all_to_all(x.reshape(NT, LEG, 1, CELLS), 'inst', 0, 0, tiled=True)  16.6 us
    all_to_all x1, starting transfers between devices, swap_rows(): y = lax.all_to_all(x.reshape(NT, LEG, 1, CELLS), 'inst', 0, 0, tiled=True)  14 us
    pallas_call x2, Pallas kernels, per_device(): pl.pallas_call(lambda *refs, last=last: update_kernel(last, *refs), out_s...  3.26 us
  transfers between devices with their start and end apart: 1, of which 1 were waited for; matrix products, arithmetic and copies ran while one was open for 0% of the time, Pallas kernels for 0%

profile of v3, /device:TPU:6, one launch (start us, length us, event | category | flops | bytes accessed | tf_op | source)
XLA Modules:
  0.0 137.2 jit_solution(5194726441130607430)
XLA Ops:
  0.0 0.0 copy-start.7
  0.0 0.0 copy-start.8
  0.0 1.0 copy.32
  1.0 0.0 copy-start.9
  1.0 0.0 copy-start.5
  1.0 0.7 copy-done.5
  1.7 1.5 %pack.1 = (f32[768,128]{1,0:T(8,128)S(1)}, f32[400,128]{1,0:T(8,128)}) custom-call(f32[384,128]{1,0:T(8,128)S(1)} %bitcast.28, s32[2,32]{1,0:T(2,128)S(1)} %bitcast.40), custom_call_target="tpu_custom_call" | custom-call | tf_op jit(solution)/shard_map/pack/pallas_call | solution.py:176
  3.1 16.6 %all_to_all.30 = f32[32,24,128]{2,1,0:T(8,128)S(1)} all-to-all(f32[32,24,128]{2,1,0:T(8,128)S(1)} %bitcast.39), channel_id=1, replica_groups=mesh['inst'=16,'mesh'=32] {'mesh'}, dimensions={0} | all-to-all | bytes 786432 | tf_op jit(solution)/shard_map/all_to_all | solution.py:138
  19.7 0.0 copy-start
  19.7 0.0 copy-start.1
  19.7 0.0 copy-start.2
  19.7 0.0 copy-start.3
  19.7 0.0 copy-start.4
  19.7 0.0 copy-start.6
  19.7 0.0 copy-start.10
  19.8 0.0 copy-start.11
  19.8 0.0 copy-done.7
  19.8 0.0 copy-done.8
  19.8 1.8 %mix.2 = f32[400,128]{1,0:T(8,128)} custom-call(f32[400,128]{1,0:T(8,128)} %get-tuple-element.11.legs, f32[768,128]{1,0:T(8,128)S(1)} %bitcast.19, s32[2,2]{1,0:T(2,128)S(1)} %copy-done.7, f32[2,2]{1,0:T(2,128)S(1)} %copy-done.8), custom_call_target="tpu_custom_call", output_to_operand_aliasing={{}: (0, {})} | custom-call | tf_op jit(solution)/shard_map/mix/pallas_call | solution.py:187
  21.6 14.0 %all-to-all-start.1 = ((f32[16,25,1,128]{3,2,1,0:T(1,128)}), f32[16,25,1,128]{3,2,1,0:T(1,128)S(1)}, u32[]{:S(2)}, u32[]{:S(2)}) async-start(f32[16,25,1,128]{3,2,1,0:T(1,128)} %bitcast.7), calls=%async_computation.1 | async-start | bytes 409600 | tf_op jit(solution)/shard_map/all_to_all | solution.py:143
  35.6 16.6 %all-to-all-done.1 = f32[16,25,1,128]{3,2,1,0:T(1,128)S(1)} async-done(((f32[16,25,1,128]{3,2,1,0:T(1,128)}), f32[16,25,1,128]{3,2,1,0:T(1,128)S(1)}, u32[]{:S(2)}, u32[]{:S(2)}) %all-to-all-start.1) | async-done | bytes 204832 | tf_op jit(solution)/shard_map/all_to_all | solution.py:143
  52.2 0.0 copy-done.9
  52.2 0.8 spectral.2
  52.9 22.2 %all_to_all.31 = f32[16,25,1,128]{3,2,1,0:T(1,128)S(1)} all-to-all(f32[16,25,1,128]{3,2,1,0:T(1,128)S(1)} %bitcast.33), channel_id=1, replica_groups=mesh['inst'=16,'mesh'=32] {'inst'}, dimensions={0} | all-to-all | bytes 409600 | tf_op jit(solution)/shard_map/all_to_all | solution.py:143
  75.1 0.0 copy-done
  75.1 0.0 copy-done.1
  75.1 0.0 copy-done.2
  75.1 0.0 copy-done.3
  75.1 0.0 copy-done.4
  75.1 0.0 copy-done.6
  75.1 0.0 copy-done.10
  75.2 0.0 copy-done.11
  75.2 1.5 %update.2 = (f32[384,128]{1,0:T(8,128)S(1)}, f32[768,128]{1,0:T(8,128)S(1)}, f32[400,128]{1,0:T(8,128)S(1)}) custom-call(f32[384,128]{1,0:T(8,128)S(1)} %bitcast.29, f32[384,128]{1,0:T(8,128)S(1)} %bitcast.37, f32[1152,128]{1,0:T(8,128)S(1)} %bitcast.30, f32[2304,128]{1,0:T(8,128)S(1)} %bitcast.22, ...), custom_call_target="tpu_custom_call", output_to_operand_aliasing={{0}: (0, {}), {1}: (8, {}), {2}: (9, {})} | custom-call | tf_op jit(solution)/shard_map/update/pallas_call | solution.py:216
  76.6 13.2 %all_to_all.32 = f32[32,24,128]{2,1,0:T(8,128)S(1)} all-to-all(f32[32,24,128]{2,1,0:T(8,128)S(1)} %bitcast.21), channel_id=1, replica_groups=mesh['inst'=16,'mesh'=32] {'mesh'}, dimensions={0} | all-to-all | bytes 786432 | tf_op jit(solution)/shard_map/all_to_all | solution.py:138
  89.8 0.6 mix.3
  90.4 22.1 %all_to_all.33 = f32[16,25,1,128]{3,2,1,0:T(1,128)S(1)} all-to-all(f32[16,25,1,128]{3,2,1,0:T(1,128)S(1)} %bitcast.27), channel_id=1, replica_groups=mesh['inst'=16,'mesh'=32] {'inst'}, dimensions={0} | all-to-all | bytes 409600 | tf_op jit(solution)/shard_map/all_to_all | solution.py:143
  112.5 0.8 spectral.3
  113.3 22.2 %all_to_all.34 = f32[16,25,1,128]{3,2,1,0:T(1,128)S(1)} all-to-all(f32[16,25,1,128]{3,2,1,0:T(1,128)S(1)} %bitcast.35), channel_id=1, replica_groups=mesh['inst'=16,'mesh'=32] {'inst'}, dimensions={0} | all-to-all | bytes 409600 | tf_op jit(solution)/shard_map/all_to_all | solution.py:143
  135.5 1.8 %update.3 = f32[384,128]{1,0:T(8,128)} custom-call(f32[384,128]{1,0:T(8,128)S(1)} %get-tuple-element.12.refs_0_, f32[384,128]{1,0:T(8,128)S(1)} %bitcast.38, f32[1152,128]{1,0:T(8,128)S(1)} %bitcast.31, f32[2304,128]{1,0:T(8,128)S(1)} %bitcast.23, f32[64,128]{1,0:T(8,128)S(1)} %copy-done.3, s32[64]{0:T(128)S(1)} %copy-done.10, s32[64]{0:T(128)S(1)} %copy-done.11, ...), custom_call_target="tpu_custom_call" | custom-call | tf_op jit(solution)/shard_map/update/pallas_call | solution.py:216
Async XLA Ops:
  0.0 19.8 %copy-start.7 = (s32[2,2]{1,0:T(2,128)S(1)}, s32[2,2]{1,0:T(2,128)}, u32[]{:S(2)}) copy-start(s32[2,2]{1,0:T(2,128)} %donor.3) | copy-start | bytes 52
  0.0 19.8 %copy-start.8 = (f32[2,2]{1,0:T(2,128)S(1)}, f32[2,2]{1,0:T(2,128)}, u32[]{:S(2)}) copy-start(f32[2,2]{1,0:T(2,128)} %weight.3) | copy-start | bytes 52
  1.0 51.2 %copy-start.9 = (s32[2]{0:T(128)S(1)}, s32[2]{0:T(128)}, u32[]{:S(2)}) copy-start(s32[2]{0:T(128)} %shift.3) | copy-start | bytes 28
  1.0 0.7 copy-start.5
  19.7 55.4 %copy-start = (f32[1,6,6,64,128]{4,3,2,1,0:T(8,128)S(1)}, f32[1,6,6,64,128]{4,3,2,1,0:T(8,128)}, u32[]{:S(2)}) copy-start(f32[1,6,6,64,128]{4,3,2,1,0:T(8,128)} %param.15) | copy-start | bytes 3538948
  19.7 55.4 %copy-start.1 = (f32[3,1,6,64,128]{4,3,2,1,0:T(8,128)S(1)}, f32[3,1,6,64,128]{4,3,2,1,0:T(8,128)}, u32[]{:S(2)}) copy-start(f32[3,1,6,64,128]{4,3,2,1,0:T(8,128)} %param.14) | copy-start | bytes 1769476
  19.7 55.4 %copy-start.2 = (f32[1,6,64,128]{3,2,1,0:T(8,128)S(1)}, f32[1,6,64,128]{3,2,1,0:T(8,128)}, u32[]{:S(2)}) copy-start(f32[1,6,64,128]{3,2,1,0:T(8,128)} %param.13) | copy-start | bytes 589828
  19.7 55.4 %copy-start.3 = (f32[64,128]{1,0:T(8,128)S(1)}, f32[64,128]{1,0:T(8,128)}, u32[]{:S(2)}) copy-start(f32[64,128]{1,0:T(8,128)} %refs_4_.3) | copy-start | bytes 98308
  19.7 55.4 %copy-start.4 = (f32[2,128]{1,0:T(2,128)S(1)}, f32[2,128]{1,0:T(2,128)}, u32[]{:S(2)}) copy-start(f32[2,128]{1,0:T(2,128)} %refs_7_.3) | copy-start | bytes 3076
  19.7 55.4 %copy-start.6 = (s32[32,2]{0,1:T(2,128)S(1)}, s32[32,2]{0,1:T(2,128)}, u32[]{:S(2)}) copy-start(s32[32,2]{0,1:T(2,128)} %param.18) | copy-start | bytes 772
  19.7 55.4 %copy-start.10 = (s32[64]{0:T(128)S(1)}, s32[64]{0:T(128)}, u32[]{:S(2)}) copy-start(s32[64]{0:T(128)} %refs_5_.3) | copy-start | bytes 772
  19.8 55.4 %copy-start.11 = (s32[64]{0:T(128)S(1)}, s32[64]{0:T(128)}, u32[]{:S(2)}) copy-start(s32[64]{0:T(128)} %refs_6_.3) | copy-start | bytes 772
  21.6 30.6 %all-to-all-start.1 = ((f32[16,25,1,128]{3,2,1,0:T(1,128)}), f32[16,25,1,128]{3,2,1,0:T(1,128)S(1)}, u32[]{:S(2)}, u32[]{:S(2)}) async-start(f32[16,25,1,128]{3,2,1,0:T(1,128)} %bitcast.7), calls=%async_computation.1 | async-start | bytes 409600 | tf_op jit(solution)/shard_map/all_to_all | solution.py:143

commit v4 on v3

--- a/solution.py
+++ b/solution.py
@@ -16,6 +16,7 @@
 SLOT = 4 * NV
 LEG = PIECE + 1
 SWEEPS = 2
+STALL = (700, 700)
 F32 = jnp.float32
 
 
@@ -30,6 +31,8 @@
 
 
 TABLE = circulant_row()
+EVEN = [0.5 * (TABLE[k] + TABLE[(k + NT // 2) % NT]) for k in range(NT)]
+ODD = [0.5 * (TABLE[k] - TABLE[(k + NT // 2) % NT]) for k in range(NT)]
 
 
 def pack_blocks(field, send, out):
@@ -42,15 +45,15 @@
             out[pl.ds(dst * SLOT + (2 + b) * NV, NV), :] = faces[b]
 
 
-def pack_kernel(field, send, out, legs):
+def pack_kernel(field, send, out):
     pack_blocks(field, send, out)
+
+
+def mix_kernel(stall, legs, field, blocks, donor, weight, place, out, spin):
     for p in range(NT):
-        legs[pl.ds(p * LEG, PIECE), :] = field[pl.ds(p * PIECE, PIECE), :]
-        legs[pl.ds(p * LEG + PIECE, 1), :] = jnp.zeros((1, CELLS), F32)
-
-
-def mix_kernel(legs, blocks, donor, weight, out):
-    out[...] = legs[...]
+        out[pl.ds(p * LEG, PIECE), :] = field[pl.ds(p * PIECE, PIECE), :]
+    for p in range(2 * NV, NT):
+        out[pl.ds(p * LEG + PIECE, 1), :] = jnp.zeros((1, CELLS), F32)
     for j in range(2):
         total = None
         for k in range(2):
@@ -60,16 +63,24 @@
             total = part if total is None else total + part
         for v in range(NV):
             out[pl.ds((j * NV + v) * LEG + PIECE, 1), :] = total[v : v + 1]
+    turns = jnp.where(place[1] % 2 == 0, stall, 0)
+    spin[...] = lax.fori_loop(0, turns, lambda i, x: pltpu.roll(x, 1, 1), field[pl.ds(0, 8), :])
 
 
 def spectral_kernel(legs, shift, inst, out):
+    half = NT // 2
     for t in range(PIECE // 8):
         rows = [legs[pl.ds(m * LEG + t * 8, 8), :] for m in range(NT)]
-        for n in range(NT):
-            acc = rows[0] * TABLE[n % NT]
-            for m in range(1, NT):
-                acc = acc + rows[m] * TABLE[(n - m) % NT]
-            out[pl.ds(n * LEG + t * 8, 8), :] = acc
+        plus = [rows[m] + rows[m + half] for m in range(half)]
+        minus = [rows[m] - rows[m + half] for m in range(half)]
+        for n in range(half):
+            a = plus[0] * EVEN[n]
+            b = minus[0] * ODD[n]
+            for m in range(1, half):
+                a = a + plus[m] * EVEN[(n - m) % NT]
+                b = b + minus[m] * ODD[(n - m) % NT]
+            out[pl.ds(n * LEG + t * 8, 8), :] = a + b
+            out[pl.ds((n + half) * LEG + t * 8, 8), :] = a - b
     turn = jnp.where(inst[0] < NV, shift[0], shift[1])
     mixes = legs[pl.ds(PIECE, NT, stride=LEG), :]
     out[pl.ds(PIECE, NT, stride=LEG), :] = pltpu.roll(mixes, NT - turn, 0)
@@ -79,7 +90,7 @@
     if last:
         out, halo, freq = rest
     else:
-        send, out, packed, legs, halo, freq = rest
+        send, fresh, out, packed, halo, freq = rest
     for b in range(BLK):
         slot = recv[b]
         row = (slot // 2) * SLOT + (slot % 2) * NV
@@ -113,10 +124,7 @@
                 new = new + jac[pl.ds((v * NV + w) * BLK + t * 8, 8), :] * total[w]
             if v == NV - 1:
                 new = jnp.maximum(new, 0.0)
-            r = v * BLK + t * 8
-            out[pl.ds(r, 8), :] = new
-            if not last:
-                legs[pl.ds((r // PIECE) * LEG + r % PIECE, 8), :] = new
+            out[pl.ds(v * BLK + t * 8, 8), :] = new
     if not last:
         pack_blocks(out, send, packed)
 
@@ -159,40 +167,43 @@
     phase_shift,
 ):
     near = lambda x: pltpu.with_memory_space_constraint(x, pltpu.VMEM)
-    small = lambda x: x
+    far = lambda x: pltpu.with_memory_space_constraint(x, pltpu.HBM)
     field = state.reshape(ROWS, CELLS)
     right = near(right_side.reshape(ROWS, CELLS))
     coup = near(couplings.reshape(3 * ROWS, CELLS))
     jac = near(jac_corr.reshape(NV * ROWS, CELLS))
     spec = near(spec_scale)
-    send = small(send_index.T)
-    inst = small(lax.axis_index("inst").astype(jnp.int32).reshape(1))
-    donor = small(donor_index)
-    weight = small(donor_weight)
-    shift = small(phase_shift)
-    recv = small(recv_slot)
-    blade = small(row_id)
-
-    packed, legs = pl.pallas_call(
+    send = send_index.T
+    place = jnp.stack([lax.axis_index("inst"), lax.axis_index("mesh")]).astype(jnp.int32)
+    donor = donor_index
+    weight = donor_weight
+    shift = phase_shift
+    recv = recv_slot
+    blade = row_id
+
+    packed = pl.pallas_call(
         pack_kernel,
-        out_shape=[rows_of(NMESH * SLOT), rows_of(NT * LEG)],
+        out_shape=rows_of(NMESH * SLOT),
         in_specs=[vmem(), smem()],
-        out_specs=[vmem()] * 2,
+        out_specs=vmem(),
         name="pack",
         compiler_params=pltpu.CompilerParams(vmem_limit_bytes=8 << 20),
-    )(near(field), send)
+    )(far(field), far(send))
+    fresh = jnp.zeros((ROWS, CELLS), F32)
+    legs = jnp.zeros((NT * LEG, CELLS), F32)
     for sweep in range(SWEEPS):
         last = sweep == SWEEPS - 1
         blocks = near(swap(packed, "mesh", NMESH))
         legs = pl.pallas_call(
-            mix_kernel,
+            lambda *refs, sweep=sweep: mix_kernel(STALL[sweep], *refs),
             out_shape=rows_of(NT * LEG),
-            in_specs=[vmem(), vmem(), smem(), smem()],
+            in_specs=[vmem(), vmem(), vmem(), smem(), smem(), smem()],
             out_specs=vmem(),
+            scratch_shapes=[pltpu.VMEM((8, CELLS), F32)],
             input_output_aliases={0: 0},
             name="mix",
             compiler_params=pltpu.CompilerParams(vmem_limit_bytes=8 << 20),
-        )(near(legs), blocks, donor, weight)
+        )(near(legs), near(field), blocks, donor, weight, place)
         legs = near(swap_rows(legs))
         back = pl.pallas_call(
             spectral_kernel,
@@ -202,17 +213,17 @@
             input_output_aliases={0: 0},
             name="spectral",
             compiler_params=pltpu.CompilerParams(vmem_limit_bytes=8 << 20),
-        )(legs, shift, inst)
+        )(legs, shift, place)
         back = near(swap_rows(back))
         ins = [near(field), right, coup, jac, spec, blade, recv, iface_coef, blocks, back]
         specs = [vmem(), vmem(), vmem(), vmem(), vmem(), smem(), smem(), vmem(), vmem(), vmem()]
         shapes = [rows_of(ROWS)]
         alias = {}
         if not last:
-            ins.append(send)
-            specs.append(smem())
-            shapes += [rows_of(NMESH * SLOT), rows_of(NT * LEG)]
-            alias = {0: 0, 8: 1, 9: 2}
+            ins += [send, near(fresh)]
+            specs += [smem(), vmem()]
+            shapes.append(rows_of(NMESH * SLOT))
+            alias = {11: 0, 8: 1}
         res = pl.pallas_call(
             lambda *refs, last=last: update_kernel(last, *refs),
             out_shape=shapes,
@@ -225,7 +236,7 @@
         )(*ins)
         field = res[0]
         if not last:
-            packed, legs = res[1], res[2]
+            packed, legs = res[1], back
     return field.reshape(1, NV, BLK, CELLS)
 
 

time: 139 us -> 132 us (0.950)
  waiting for transfers between devices: 16.6 us -> 8.03 us
  Pallas kernels: 8.62 us -> 15.1 us
  starting transfers between devices: 14 us -> 9.52 us
  blocking collectives: 96.2 us -> 98.3 us
  local copies, waits for them, and re-layouts: 1.7 us -> 0.09 us
    all_to_all x3 -> x4, blocking collectives: 66.5 us -> 85.1 us  [swap_rows(): y = lax.all_to_all(x.reshape(NT, LEG, 1, CELLS), 'inst', 0, 0, tiled=True)]
    all_to_all x2 -> x1, blocking collectives: 29.8 us -> 13.2 us  [swap(): lax.all_to_all(x.reshape(parts, rows // parts, CELLS), axis, 0, 0, tiled=...]
    all_to_all x1, waiting for transfers between devices: 16.6 us -> 8.03 us  [swap(): lax.all_to_all(x.reshape(parts, rows // parts, CELLS), axis, 0, 0, tiled=...]
    pallas_call x3, Pallas kernels: 3.86 us -> 10.5 us  [the longest x2 8.58 us: per_device(): pl.pallas_call(lambda *refs, sweep=sweep: mix_kernel(STALL[sweep], *refs)...]
    all_to_all x1, starting transfers between devices: 14 us -> 9.52 us  [swap(): lax.all_to_all(x.reshape(parts, rows // parts, CELLS), axis, 0, 0, tiled=...]
    unnamed x25 -> x24, local copies, waits for them, and re-layouts: 1.7 us -> 0.07 us
where the time goes in v4:
time: 132 us; the launch traced here: 131 us
  blocking collectives  98.3 us (74%)
  Pallas kernels  15.1 us (11%)
  starting transfers between devices  9.52 us (7%)
  waiting for transfers between devices  8.03 us (6%)
    all_to_all x4, blocking collectives, swap_rows(): y = lax.all_to_all(x.reshape(NT, LEG, 1, CELLS), 'inst', 0, 0, tiled=True)  85.1 us
    all_to_all x1, blocking collectives, swap(): lax.all_to_all(x.reshape(parts, rows // parts, CELLS), axis, 0, 0, tiled=...  13.2 us
    all_to_all x1, starting transfers between devices, swap(): lax.all_to_all(x.reshape(parts, rows // parts, CELLS), axis, 0, 0, tiled=...  9.52 us
    pallas_call x2, Pallas kernels, per_device(): pl.pallas_call(lambda *refs, sweep=sweep: mix_kernel(STALL[sweep], *refs)...  8.58 us
    all_to_all x1, waiting for transfers between devices, swap(): lax.all_to_all(x.reshape(parts, rows // parts, CELLS), axis, 0, 0, tiled=...  8.03 us
    pallas_call x2, Pallas kernels, per_device(): pl.pallas_call(lambda *refs, last=last: update_kernel(last, *refs), out_s...  3.27 us
  transfers between devices with their start and end apart: 1, of which 1 were waited for; matrix products, arithmetic and copies ran while one was open for 0% of the time, Pallas kernels for 0%

profile of v4, /device:TPU:6, one launch (start us, length us, event | category | flops | bytes accessed | tf_op | source)
XLA Modules:
  0.0 131.4 jit_solution(17422150569572618545)
XLA Ops:
  0.0 0.0 copy-start.2
  0.0 0.0 copy-start.8
  0.0 0.0 copy-start.7
  0.0 2.0 %pack.1 = f32[768,128]{1,0:T(8,128)} custom-call(f32[384,128]{1,0:T(8,128)} %bitcast.37, s32[2,32]{1,0:T(2,128)} %bitcast.43), custom_call_target="tpu_custom_call" | custom-call | tf_op jit(solution)/shard_map/pack/pallas_call | solution.py:184
  2.0 0.0 copy-start.9
  2.0 9.5 %all-to-all-start = ((f32[32,24,128]{2,1,0:T(8,128)}), f32[32,24,128]{2,1,0:T(8,128)S(1)}, u32[]{:S(2)}, u32[]{:S(2)}) async-start(f32[32,24,128]{2,1,0:T(8,128)} %bitcast.5), calls=%async_computation | async-start | bytes 786432 | tf_op jit(solution)/shard_map/all_to_all | solution.py:146
  11.5 0.1 pad_add_fusion.refs_5_.inst
  11.6 8.0 %all-to-all-done = f32[32,24,128]{2,1,0:T(8,128)S(1)} async-done(((f32[32,24,128]{2,1,0:T(8,128)}), f32[32,24,128]{2,1,0:T(8,128)S(1)}, u32[]{:S(2)}, u32[]{:S(2)}) %all-to-all-start) | async-done | bytes 393248 | tf_op jit(solution)/shard_map/all_to_all | solution.py:146
  19.6 0.0 copy-done.2
  19.6 0.0 copy-done.8
  19.6 0.0 copy-done.7
  19.7 0.0 copy-start
  19.7 0.0 copy-start.1
  19.7 0.0 copy-start.3
  19.7 0.0 copy-start.4
  19.7 0.0 copy-start.5
  19.7 0.0 copy-start.6
  19.7 0.0 copy-start.10
  19.7 0.0 copy-start.11
  19.8 4.3 %mix.2 = f32[400,128]{1,0:T(8,128)S(1)} custom-call(f32[400,128]{1,0:T(8,128)S(1)} %broadcast_in_dim.6.refs_0_, f32[384,128]{1,0:T(8,128)S(1)} %bitcast.38, f32[768,128]{1,0:T(8,128)S(1)} %bitcast.20, s32[2,2]{1,0:T(2,128)S(1)} %copy-done.7, f32[2,2]{1,0:T(2,128)S(1)} %copy-done.8, s32[2]{0:T(128)S(1)} %pad_add_fusion.refs_5_.inst), custom_call_target="tpu_custom_call", output_to_operand_aliasing={{}: (0, {})} | custom-call | tf_op jit(solution)/shard_map/mix/pallas_call | solution.py:197
  24.1 28.5 %all_to_all.30 = f32[16,25,1,128]{3,2,1,0:T(1,128)S(1)} all-to-all(f32[16,25,1,128]{3,2,1,0:T(1,128)S(1)} %bitcast.32), channel_id=1, replica_groups=mesh['inst'=16,'mesh'=32] {'inst'}, dimensions={0} | all-to-all | bytes 409600 | tf_op jit(solution)/shard_map/all_to_all | solution.py:151
  52.6 0.0 copy-done.9
  52.6 0.7 spectral.2
  53.3 18.5 %all_to_all.31 = f32[16,25,1,128]{3,2,1,0:T(1,128)S(1)} all-to-all(f32[16,25,1,128]{3,2,1,0:T(1,128)S(1)} %bitcast.36), channel_id=1, replica_groups=mesh['inst'=16,'mesh'=32] {'inst'}, dimensions={0} | all-to-all | bytes 409600 | tf_op jit(solution)/shard_map/all_to_all | solution.py:151
  71.8 0.0 copy-done
  71.8 0.0 copy-done.1
  71.8 0.0 copy-done.3
  71.8 0.0 copy-done.4
  71.8 0.0 copy-done.5
  71.8 0.0 copy-done.6
  71.8 0.0 copy-done.10
  71.8 0.0 copy-done.11
  71.8 1.5 %update.2 = (f32[384,128]{1,0:T(8,128)S(1)}, f32[768,128]{1,0:T(8,128)S(1)}) custom-call(f32[384,128]{1,0:T(8,128)S(1)} %bitcast.39, f32[384,128]{1,0:T(8,128)S(1)} %bitcast.41, f32[1152,128]{1,0:T(8,128)S(1)} %bitcast.30, f32[2304,128]{1,0:T(8,128)S(1)} %bitcast.23, f32[64,128]{1,0:T(8,128)S(1)} %copy-done.4, ...), custom_call_target="tpu_custom_call", output_to_operand_aliasing={{0}: (11, {}), {1}: (8, {})} | custom-call | tf_op jit(solution)/shard_map/update/pallas_call | solution.py:227
  73.3 13.2 %all_to_all.32 = f32[32,24,128]{2,1,0:T(8,128)S(1)} all-to-all(f32[32,24,128]{2,1,0:T(8,128)S(1)} %bitcast.22), channel_id=1, replica_groups=mesh['inst'=16,'mesh'=32] {'mesh'}, dimensions={0} | all-to-all | bytes 786432 | tf_op jit(solution)/shard_map/all_to_all | solution.py:146
  86.5 4.3 %mix.3 = f32[400,128]{1,0:T(8,128)S(1)} custom-call(f32[400,128]{1,0:T(8,128)S(1)} %bitcast.28, f32[384,128]{1,0:T(8,128)S(1)} %get-tuple-element.7.refs_1_.refs_0_, f32[768,128]{1,0:T(8,128)S(1)} %bitcast.25, s32[2,2]{1,0:T(2,128)S(1)} %copy-done.7, f32[2,2]{1,0:T(2,128)S(1)} %copy-done.8, ...), custom_call_target="tpu_custom_call", output_to_operand_aliasing={{}: (0, {})} | custom-call | tf_op jit(solution)/shard_map/mix/pallas_call | solution.py:197
  90.8 19.6 %all_to_all.33 = f32[16,25,1,128]{3,2,1,0:T(1,128)S(1)} all-to-all(f32[16,25,1,128]{3,2,1,0:T(1,128)S(1)} %bitcast.29), channel_id=1, replica_groups=mesh['inst'=16,'mesh'=32] {'inst'}, dimensions={0} | all-to-all | bytes 409600 | tf_op jit(solution)/shard_map/all_to_all | solution.py:151
  110.4 0.7 spectral.3
  111.1 18.5 %all_to_all.34 = f32[16,25,1,128]{3,2,1,0:T(1,128)S(1)} all-to-all(f32[16,25,1,128]{3,2,1,0:T(1,128)S(1)} %bitcast.34), channel_id=1, replica_groups=mesh['inst'=16,'mesh'=32] {'inst'}, dimensions={0} | all-to-all | bytes 409600 | tf_op jit(solution)/shard_map/all_to_all | solution.py:151
  129.6 1.8 %update.3 = f32[384,128]{1,0:T(8,128)} custom-call(f32[384,128]{1,0:T(8,128)S(1)} %get-tuple-element.7.refs_1_.refs_0_, f32[384,128]{1,0:T(8,128)S(1)} %bitcast.42, f32[1152,128]{1,0:T(8,128)S(1)} %bitcast.31, f32[2304,128]{1,0:T(8,128)S(1)} %bitcast.24, f32[64,128]{1,0:T(8,128)S(1)} %copy-done.4, s32[64]{0:T(128)S(1)} %copy-done.10, s32[64]{0:T(128)S(1)} %copy-done.11, ...), custom_call_target="tpu_custom_call" | custom-call | tf_op jit(solution)/shard_map/update/pallas_call | solution.py:227
  (2 shorter events, 0.0 us)
Async XLA Ops:
  0.0 19.6 %copy-start.2 = (f32[1,6,64,128]{3,2,1,0:T(8,128)S(1)}, f32[1,6,64,128]{3,2,1,0:T(8,128)}, u32[]{:S(2)}) copy-start(f32[1,6,64,128]{3,2,1,0:T(8,128)} %param.12) | copy-start | bytes 589828
  0.0 19.6 %copy-start.8 = (f32[2,2]{1,0:T(2,128)S(1)}, f32[2,2]{1,0:T(2,128)}, u32[]{:S(2)}) copy-start(f32[2,2]{1,0:T(2,128)} %refs_4_.6) | copy-start | bytes 52
  0.0 19.6 %copy-start.7 = (s32[2,2]{1,0:T(2,128)S(1)}, s32[2,2]{1,0:T(2,128)}, u32[]{:S(2)}) copy-start(s32[2,2]{1,0:T(2,128)} %refs_3_.3) | copy-start | bytes 52
  2.0 50.6 %copy-start.9 = (s32[2]{0:T(128)S(1)}, s32[2]{0:T(128)}, u32[]{:S(2)}) copy-start(s32[2]{0:T(128)} %shift.3) | copy-start | bytes 28
  2.0 17.6 %all-to-all-start = ((f32[32,24,128]{2,1,0:T(8,128)}), f32[32,24,128]{2,1,0:T(8,128)S(1)}, u32[]{:S(2)}, u32[]{:S(2)}) async-start(f32[32,24,128]{2,1,0:T(8,128)} %bitcast.5), calls=%async_computation | async-start | bytes 786432 | tf_op jit(solution)/shard_map/all_to_all | solution.py:146
  19.7 52.1 %copy-start = (f32[1,6,6,64,128]{4,3,2,1,0:T(8,128)S(1)}, f32[1,6,6,64,128]{4,3,2,1,0:T(8,128)}, u32[]{:S(2)}) copy-start(f32[1,6,6,64,128]{4,3,2,1,0:T(8,128)} %param.15) | copy-start | bytes 3538948
  19.7 52.1 %copy-start.1 = (f32[3,1,6,64,128]{4,3,2,1,0:T(8,128)S(1)}, f32[3,1,6,64,128]{4,3,2,1,0:T(8,128)}, u32[]{:S(2)}) copy-start(f32[3,1,6,64,128]{4,3,2,1,0:T(8,128)} %param.14) | copy-start | bytes 1769476
  19.7 52.1 %copy-start.3 = (f32[1,6,64,128]{3,2,1,0:T(8,128)S(1)}, f32[1,6,64,128]{3,2,1,0:T(8,128)}, u32[]{:S(2)}) copy-start(f32[1,6,64,128]{3,2,1,0:T(8,128)} %param.13) | copy-start | bytes 589828
  19.7 52.1 %copy-start.4 = (f32[64,128]{1,0:T(8,128)S(1)}, f32[64,128]{1,0:T(8,128)}, u32[]{:S(2)}) copy-start(f32[64,128]{1,0:T(8,128)} %refs_4_.7) | copy-start | bytes 98308
  19.7 52.1 %copy-start.5 = (f32[2,128]{1,0:T(2,128)S(1)}, f32[2,128]{1,0:T(2,128)}, u32[]{:S(2)}) copy-start(f32[2,128]{1,0:T(2,128)} %refs_7_.3) | copy-start | bytes 3076
  19.7 52.1 %copy-start.6 = (s32[32,2]{0,1:T(2,128)S(1)}, s32[32,2]{0,1:T(2,128)}, u32[]{:S(2)}) copy-start(s32[32,2]{0,1:T(2,128)} %param.18) | copy-start | bytes 772
  19.7 52.1 %copy-start.10 = (s32[64]{0:T(128)S(1)}, s32[64]{0:T(128)}, u32[]{:S(2)}) copy-start(s32[64]{0:T(128)} %refs_5_.3) | copy-start | bytes 772
  19.7 52.1 %copy-start.11 = (s32[64]{0:T(128)S(1)}, s32[64]{0:T(128)}, u32[]{:S(2)}) copy-start(s32[64]{0:T(128)} %refs_6_.3) | copy-start | bytes 772

commit v5 on v4

--- a/solution.py
+++ b/solution.py
@@ -16,7 +16,7 @@
 SLOT = 4 * NV
 LEG = PIECE + 1
 SWEEPS = 2
-STALL = (700, 700)
+STALL = (560, 560)
 F32 = jnp.float32
 
 
@@ -45,11 +45,33 @@
             out[pl.ds(dst * SLOT + (2 + b) * NV, NV), :] = faces[b]
 
 
-def pack_kernel(field, send, out):
+def pack_kernel(field, send, place, out_in, out):
     pack_blocks(field, send, out)
 
 
-def mix_kernel(stall, legs, field, blocks, donor, weight, place, out, spin):
+def local_terms(field, right, coup, spec, row_id, recv, blocks, part, freq, halo):
+    for b in range(BLK):
+        slot = recv[b]
+        row = (slot // 2) * SLOT + (slot % 2) * NV
+        halo[pl.ds(b, NV, stride=BLK), :] = blocks[pl.ds(row, NV), :]
+        freq[pl.ds(b, 1), :] = spec[pl.ds(b, 1), :] * (1.0 + 0.5 * row_id[b].astype(F32))
+    lane = lax.broadcasted_iota(jnp.int32, (8, CELLS), 1)
+    not_first = lane > 0
+    not_last = lane < CELLS - 1
+    for t in range(ROWS // 8):
+        r = t * 8
+        here = field[pl.ds(r, 8), :]
+        below = jnp.where(not_first, pltpu.roll(here, 1, 1), 0.0)
+        above = jnp.where(not_last, pltpu.roll(here, CELLS - 1, 1), 0.0)
+        val = right[pl.ds(r, 8), :]
+        val = val + (coup[pl.ds(r, 8), :] * below + coup[pl.ds(ROWS + r, 8), :] * above)
+        part[pl.ds(r, 8), :] = val + coup[pl.ds(2 * ROWS + r, 8), :] * halo[pl.ds(r, 8), :]
+
+
+def mix_kernel(
+    stall, legs, donor, weight, place, field, right, coup, spec, row_id, recv, blocks, part_in, freq_in,
+    out, part, freq, halo, spin,
+):
     for p in range(NT):
         out[pl.ds(p * LEG, PIECE), :] = field[pl.ds(p * PIECE, PIECE), :]
     for p in range(2 * NV, NT):
@@ -59,12 +81,14 @@
         for k in range(2):
             who = donor[j, k]
             row = (who // 2) * SLOT + (2 + who % 2) * NV
-            part = blocks[pl.ds(row, NV), :] * weight[j, k]
-            total = part if total is None else total + part
+            face = blocks[pl.ds(row, NV), :] * weight[j, k]
+            total = face if total is None else total + face
         for v in range(NV):
             out[pl.ds((j * NV + v) * LEG + PIECE, 1), :] = total[v : v + 1]
-    turns = jnp.where(place[1] % 2 == 0, stall, 0)
-    spin[...] = lax.fori_loop(0, turns, lambda i, x: pltpu.roll(x, 1, 1), field[pl.ds(0, 8), :])
+    @pl.when(place[1] % 2 == 0)
+    def _():
+        local_terms(field, right, coup, spec, row_id, recv, blocks, part, freq, halo)
+        spin[...] = lax.fori_loop(0, stall, lambda i, x: pltpu.roll(x, 1, 1), field[pl.ds(0, 8), :])
 
 
 def spectral_kernel(legs, shift, inst, out):
@@ -86,33 +110,31 @@
     out[pl.ds(PIECE, NT, stride=LEG), :] = pltpu.roll(mixes, NT - turn, 0)
 
 
-def update_kernel(last, field, right, coup, jac, spec, row_id, recv, coef, blocks, back, *rest):
+def update_kernel(
+    last, part_in, freq_in, jac, coef, place, back, field, right, coup, spec, row_id, recv, blocks, *rest
+):
     if last:
-        out, halo, freq = rest
+        out, part, freq, halo = rest
     else:
-        send, fresh, out, packed, halo, freq = rest
-    for b in range(BLK):
-        slot = recv[b]
-        row = (slot // 2) * SLOT + (slot % 2) * NV
-        halo[pl.ds(b, NV, stride=BLK), :] = blocks[pl.ds(row, NV), :]
-        freq[pl.ds(b, 1), :] = spec[pl.ds(b, 1), :] * (1.0 + 0.5 * row_id[b].astype(F32))
-    lane = lax.broadcasted_iota(jnp.int32, (8, CELLS), 1)
+        send, fresh, out, packed, part, freq, halo = rest
+
+    @pl.when(place[1] % 2 == 0)
+    def _():
+        part[...] = part_in[...]
+        freq[...] = freq_in[...]
+
+    @pl.when(place[1] % 2 == 1)
+    def _():
+        local_terms(field, right, coup, spec, row_id, recv, blocks, part, freq, halo)
+
     sub = lax.broadcasted_iota(jnp.int32, (8, CELLS), 0)
-    not_first = lane > 0
-    not_last = lane < CELLS - 1
     for t in range(BLK // 8):
         total = []
         f = freq[pl.ds(t * 8, 8), :]
         for v in range(NV):
             r = v * BLK + t * 8
-            here = field[pl.ds(r, 8), :]
-            below = jnp.where(not_first, pltpu.roll(here, 1, 1), 0.0)
-            above = jnp.where(not_last, pltpu.roll(here, CELLS - 1, 1), 0.0)
             p, q = r // PIECE, r % PIECE
-            val = right[pl.ds(r, 8), :]
-            val = val + (coup[pl.ds(r, 8), :] * below + coup[pl.ds(ROWS + r, 8), :] * above)
-            val = val + coup[pl.ds(2 * ROWS + r, 8), :] * halo[pl.ds(r, 8), :]
-            val = val - f * back[pl.ds(p * LEG + q, 8), :]
+            val = part[pl.ds(r, 8), :] - f * back[pl.ds(p * LEG + q, 8), :]
             if t == 0:
                 for j in range(2):
                     mix = coef[pl.ds(j, 1), :] * back[pl.ds((j * NV + v) * LEG + PIECE, 1), :]
@@ -184,26 +206,31 @@
     packed = pl.pallas_call(
         pack_kernel,
         out_shape=rows_of(NMESH * SLOT),
-        in_specs=[vmem(), smem()],
+        in_specs=[vmem(), smem(), smem(), vmem()],
         out_specs=vmem(),
+        input_output_aliases={3: 0},
         name="pack",
         compiler_params=pltpu.CompilerParams(vmem_limit_bytes=8 << 20),
-    )(far(field), far(send))
+    )(far(field), far(send), place, near(jnp.zeros((NMESH * SLOT, CELLS), F32)))
     fresh = jnp.zeros((ROWS, CELLS), F32)
+    part = jnp.zeros((ROWS, CELLS), F32)
+    freq = jnp.zeros((BLK, CELLS), F32)
     legs = jnp.zeros((NT * LEG, CELLS), F32)
     for sweep in range(SWEEPS):
         last = sweep == SWEEPS - 1
         blocks = near(swap(packed, "mesh", NMESH))
-        legs = pl.pallas_call(
+        near_by = [near(field), right, coup, spec, blade, recv, blocks]
+        near_specs = [vmem(), vmem(), vmem(), vmem(), smem(), smem(), vmem()]
+        legs, part, freq = pl.pallas_call(
             lambda *refs, sweep=sweep: mix_kernel(STALL[sweep], *refs),
-            out_shape=rows_of(NT * LEG),
-            in_specs=[vmem(), vmem(), vmem(), smem(), smem(), smem()],
-            out_specs=vmem(),
-            scratch_shapes=[pltpu.VMEM((8, CELLS), F32)],
-            input_output_aliases={0: 0},
+            out_shape=[rows_of(NT * LEG), rows_of(ROWS), rows_of(BLK)],
+            in_specs=[vmem(), smem(), smem(), smem()] + near_specs + [vmem()] * 2,
+            out_specs=[vmem()] * 3,
+            scratch_shapes=[pltpu.VMEM((ROWS, CELLS), F32), pltpu.VMEM((8, CELLS), F32)],
+            input_output_aliases={0: 0, 11: 1, 12: 2},
             name="mix",
             compiler_params=pltpu.CompilerParams(vmem_limit_bytes=8 << 20),
-        )(near(legs), near(field), blocks, donor, weight, place)
+        )(near(legs), donor, weight, place, *near_by, near(part), near(freq))
         legs = near(swap_rows(legs))
         back = pl.pallas_call(
             spectral_kernel,
@@ -215,21 +242,21 @@
             compiler_params=pltpu.CompilerParams(vmem_limit_bytes=8 << 20),
         )(legs, shift, place)
         back = near(swap_rows(back))
-        ins = [near(field), right, coup, jac, spec, blade, recv, iface_coef, blocks, back]
-        specs = [vmem(), vmem(), vmem(), vmem(), vmem(), smem(), smem(), vmem(), vmem(), vmem()]
+        ins = [near(part), near(freq), jac, iface_coef, place, back] + near_by
+        specs = [vmem()] * 4 + [smem(), vmem()] + near_specs
         shapes = [rows_of(ROWS)]
         alias = {}
         if not last:
             ins += [send, near(fresh)]
             specs += [smem(), vmem()]
             shapes.append(rows_of(NMESH * SLOT))
-            alias = {11: 0, 8: 1}
+            alias = {14: 0, 12: 1}
         res = pl.pallas_call(
             lambda *refs, last=last: update_kernel(last, *refs),
             out_shape=shapes,
             in_specs=specs,
             out_specs=[vmem()] * len(shapes),
-            scratch_shapes=[pltpu.VMEM((ROWS, CELLS), F32), pltpu.VMEM((BLK, CELLS), F32)],
+            scratch_shapes=[pltpu.VMEM((n, CELLS), F32) for n in (ROWS, BLK, ROWS)],
             input_output_aliases=alias,
             name="update",
             compiler_params=pltpu.CompilerParams(vmem_limit_bytes=8 << 20),

time: 132 us -> 131 us (level)
  blocking collectives: 98.3 us -> 117 us
  starting transfers between devices: 9.52 us -> 0 us
  waiting for transfers between devices: 8.03 us -> 0 us
  Pallas kernels: 15.1 us -> 13.2 us
    all_to_all x1 -> x2, blocking collectives: 13.2 us -> 29.7 us  [swap(): lax.all_to_all(x.reshape(parts, rows // parts, CELLS), axis, 0, 0, tiled=...]
    all_to_all x1 -> x0, starting transfers between devices: 9.52 us -> none  [swap(): lax.all_to_all(x.reshape(parts, rows // parts, CELLS), axis, 0, 0, tiled=...]
    all_to_all x1 -> x0, waiting for transfers between devices: 8.03 us -> none  [swap(): lax.all_to_all(x.reshape(parts, rows // parts, CELLS), axis, 0, 0, tiled=...]
    all_to_all x4, blocking collectives: 85.1 us -> 86.9 us  [swap_rows(): y = lax.all_to_all(x.reshape(NT, LEG, 1, CELLS), 'inst', 0, 0, tiled=True)]
  transfers between devices with their start and end apart: 1 -> 0, of which waited for: 1 -> 0; matrix products, arithmetic and copies ran while one was open for 0% -> 0% of each run, Pallas kernels for 0% -> 0%
where the time goes in v5:
time: 131 us; the launch traced here: 130 us
  blocking collectives  117 us (89%)
  Pallas kernels  13.2 us (10%)
    all_to_all x4, blocking collectives, swap_rows(): y = lax.all_to_all(x.reshape(NT, LEG, 1, CELLS), 'inst', 0, 0, tiled=True)  86.9 us
    all_to_all x2, blocking collectives, swap(): lax.all_to_all(x.reshape(parts, rows // parts, CELLS), axis, 0, 0, tiled=...  29.7 us
    pallas_call x2, Pallas kernels, per_device(): pl.pallas_call(lambda *refs, sweep=sweep: mix_kernel(STALL[sweep], *refs)...  8.24 us

profile of v5, /device:TPU:6, one launch (start us, length us, event | category | flops | bytes accessed | tf_op | source)
XLA Modules:
  0.0 130.2 jit_solution(12516716625747373874)
XLA Ops:
  0.0 0.1 pad_add_fusion.place.refs_3_.inst.refs_4_
  0.1 0.0 copy-start
  0.1 0.0 copy-start.2
  0.1 0.0 copy-start.3
  0.1 0.0 copy-start.4
  0.2 0.0 copy-start.5
  0.2 0.0 copy-start.6
  0.2 0.0 copy-start.7
  0.2 0.0 copy-start.8
  0.2 1.2 pack.1
  1.4 16.6 %all_to_all.30 = f32[32,24,128]{2,1,0:T(8,128)S(1)} all-to-all(f32[32,24,128]{2,1,0:T(8,128)S(1)} %bitcast.31), channel_id=1, replica_groups=mesh['inst'=16,'mesh'=32] {'mesh'}, dimensions={0} | all-to-all | bytes 786432 | tf_op jit(solution)/shard_map/all_to_all | solution.py:168
  18.1 0.0 copy-done
  18.1 0.0 copy-done.2
  18.1 0.0 copy-done.3
  18.1 0.0 copy-done.4
  18.1 0.0 copy-done.5
  18.1 0.0 copy-done.6
  18.1 0.0 copy-done.7
  18.2 0.0 copy-done.8
  18.2 0.0 copy-start.11
  18.2 4.1 %mix.2 = (f32[400,128]{1,0:T(8,128)S(1)}, f32[384,128]{1,0:T(8,128)S(1)}, f32[64,128]{1,0:T(8,128)S(1)}) custom-call(f32[400,128]{1,0:T(8,128)S(1)} %broadcast_in_dim.9.refs_0_, s32[2,2]{1,0:T(2,128)S(1)} %copy-done.7, f32[2,2]{1,0:T(2,128)S(1)} %copy-done.8, ...), custom_call_target="tpu_custom_call", output_to_operand_aliasing={{0}: (0, {}), {1}: (11, {}), {2}: (12, {})} | custom-call | tf_op jit(solution)/shard_map/mix/pallas_call | solution.py:224
  22.3 0.0 copy-start.1
  22.3 0.0 copy-start.9
  22.3 0.0 copy-start.10
  22.3 29.7 %all_to_all.31 = f32[16,25,1,128]{3,2,1,0:T(1,128)S(1)} all-to-all(f32[16,25,1,128]{3,2,1,0:T(1,128)S(1)} %bitcast.39), channel_id=1, replica_groups=mesh['inst'=16,'mesh'=32] {'inst'}, dimensions={0} | all-to-all | bytes 409600 | tf_op jit(solution)/shard_map/all_to_all | solution.py:173
  52.1 0.0 copy-done.11
  52.1 0.7 spectral.2
  52.7 18.5 %all_to_all.32 = f32[16,25,1,128]{3,2,1,0:T(1,128)S(1)} all-to-all(f32[16,25,1,128]{3,2,1,0:T(1,128)S(1)} %bitcast.41), channel_id=1, replica_groups=mesh['inst'=16,'mesh'=32] {'inst'}, dimensions={0} | all-to-all | bytes 409600 | tf_op jit(solution)/shard_map/all_to_all | solution.py:173
  71.3 0.0 copy-done.1
  71.3 0.0 copy-done.9
  71.3 0.0 copy-done.10
  71.3 1.0 update.2
  72.3 13.1 %all_to_all.33 = f32[32,24,128]{2,1,0:T(8,128)S(1)} all-to-all(f32[32,24,128]{2,1,0:T(8,128)S(1)} %bitcast.26), channel_id=1, replica_groups=mesh['inst'=16,'mesh'=32] {'mesh'}, dimensions={0} | all-to-all | bytes 786432 | tf_op jit(solution)/shard_map/all_to_all | solution.py:168
  85.4 4.1 %mix.3 = (f32[400,128]{1,0:T(8,128)S(1)}, f32[384,128]{1,0:T(8,128)S(1)}, f32[64,128]{1,0:T(8,128)S(1)}) custom-call(f32[400,128]{1,0:T(8,128)S(1)} %bitcast.33, s32[2,2]{1,0:T(2,128)S(1)} %copy-done.7, f32[2,2]{1,0:T(2,128)S(1)} %copy-done.8, ...), custom_call_target="tpu_custom_call", output_to_operand_aliasing={{0}: (0, {}), {1}: (11, {}), {2}: (12, {})} | custom-call | tf_op jit(solution)/shard_map/mix/pallas_call | solution.py:224
  89.5 20.1 %all_to_all.34 = f32[16,25,1,128]{3,2,1,0:T(1,128)S(1)} all-to-all(f32[16,25,1,128]{3,2,1,0:T(1,128)S(1)} %bitcast.34), channel_id=1, replica_groups=mesh['inst'=16,'mesh'=32] {'inst'}, dimensions={0} | all-to-all | bytes 409600 | tf_op jit(solution)/shard_map/all_to_all | solution.py:173
  109.6 0.7 spectral.3
  110.3 18.5 %all_to_all.35 = f32[16,25,1,128]{3,2,1,0:T(1,128)S(1)} all-to-all(f32[16,25,1,128]{3,2,1,0:T(1,128)S(1)} %bitcast.43), channel_id=1, replica_groups=mesh['inst'=16,'mesh'=32] {'inst'}, dimensions={0} | all-to-all | bytes 409600 | tf_op jit(solution)/shard_map/all_to_all | solution.py:173
  128.8 1.4 %update.3 = f32[384,128]{1,0:T(8,128)} custom-call(f32[384,128]{1,0:T(8,128)S(1)} %get-tuple-element.18.refs_0_, f32[64,128]{1,0:T(8,128)S(1)} %get-tuple-element.19.refs_1_, f32[2304,128]{1,0:T(8,128)S(1)} %bitcast.28, f32[2,128]{1,0:T(2,128)S(1)} %copy-done.9, s32[2]{0:T(128)S(1)} %pad_add_fusion.place.refs_3_.inst.refs_4_, f32[400,128]{1,0:T(8,128)S(1)} %bitcast.47, ...), custom_call_target="tpu_custom_call" | custom-call | tf_op jit(solution)/shard_map/update/pallas_call | solution.py:254
  (5 shorter events, 0.1 us)
Async XLA Ops:
  0.1 18.0 %copy-start = (f32[3,1,6,64,128]{4,3,2,1,0:T(8,128)S(1)}, f32[3,1,6,64,128]{4,3,2,1,0:T(8,128)}, u32[]{:S(2)}) copy-start(f32[3,1,6,64,128]{4,3,2,1,0:T(8,128)} %param.14) | copy-start | bytes 1769476
  0.1 18.0 %copy-start.2 = (f32[1,6,64,128]{3,2,1,0:T(8,128)S(1)}, f32[1,6,64,128]{3,2,1,0:T(8,128)}, u32[]{:S(2)}) copy-start(f32[1,6,64,128]{3,2,1,0:T(8,128)} %param.13) | copy-start | bytes 589828
  0.1 18.0 %copy-start.3 = (f32[1,6,64,128]{3,2,1,0:T(8,128)S(1)}, f32[1,6,64,128]{3,2,1,0:T(8,128)}, u32[]{:S(2)}) copy-start(f32[1,6,64,128]{3,2,1,0:T(8,128)} %param.12) | copy-start | bytes 589828
  0.1 18.0 %copy-start.4 = (f32[64,128]{1,0:T(8,128)S(1)}, f32[64,128]{1,0:T(8,128)}, u32[]{:S(2)}) copy-start(f32[64,128]{1,0:T(8,128)} %refs_9_.7) | copy-start | bytes 98308
  0.2 18.0 %copy-start.5 = (s32[64]{0:T(128)S(1)}, s32[64]{0:T(128)}, u32[]{:S(2)}) copy-start(s32[64]{0:T(128)} %refs_10_.3) | copy-start | bytes 772
  0.2 18.0 %copy-start.6 = (s32[64]{0:T(128)S(1)}, s32[64]{0:T(128)}, u32[]{:S(2)}) copy-start(s32[64]{0:T(128)} %refs_11_.3) | copy-start | bytes 772
  0.2 18.0 %copy-start.7 = (s32[2,2]{1,0:T(2,128)S(1)}, s32[2,2]{1,0:T(2,128)}, u32[]{:S(2)}) copy-start(s32[2,2]{1,0:T(2,128)} %refs_1_.3) | copy-start | bytes 52
  0.2 18.0 %copy-start.8 = (f32[2,2]{1,0:T(2,128)S(1)}, f32[2,2]{1,0:T(2,128)}, u32[]{:S(2)}) copy-start(f32[2,2]{1,0:T(2,128)} %refs_2_.3) | copy-start | bytes 52
  18.2 33.9 %copy-start.11 = (s32[2]{0:T(128)S(1)}, s32[2]{0:T(128)}, u32[]{:S(2)}) copy-start(s32[2]{0:T(128)} %shift.3) | copy-start | bytes 28
  22.3 49.0 %copy-start.1 = (f32[1,6,6,64,128]{4,3,2,1,0:T(8,128)S(1)}, f32[1,6,6,64,128]{4,3,2,1,0:T(8,128)}, u32[]{:S(2)}) copy-start(f32[1,6,6,64,128]{4,3,2,1,0:T(8,128)} %param.15) | copy-start | bytes 3538948
  22.3 49.0 %copy-start.9 = (f32[2,128]{1,0:T(2,128)S(1)}, f32[2,128]{1,0:T(2,128)}, u32[]{:S(2)}) copy-start(f32[2,128]{1,0:T(2,128)} %refs_3_.3) | copy-start | bytes 3076
  22.3 49.0 %copy-start.10 = (s32[32,2]{0,1:T(2,128)S(1)}, s32[32,2]{0,1:T(2,128)}, u32[]{:S(2)}) copy-start(s32[32,2]{0,1:T(2,128)} %param.18) | copy-start | bytes 772

commit v6 on v5

--- a/solution.py
+++ b/solution.py
@@ -16,7 +16,7 @@
 SLOT = 4 * NV
 LEG = PIECE + 1
 SWEEPS = 2
-STALL = (560, 560)
+STALL = (700, 560)
 F32 = jnp.float32
 
 
@@ -107,7 +107,7 @@
             out[pl.ds((n + half) * LEG + t * 8, 8), :] = a - b
     turn = jnp.where(inst[0] < NV, shift[0], shift[1])
     mixes = legs[pl.ds(PIECE, NT, stride=LEG), :]
-    out[pl.ds(PIECE, NT, stride=LEG), :] = pltpu.roll(mixes, NT - turn, 0)
+    out[pl.ds(PIECE, NT, stride=LEG), :] = pltpu.roll(mixes, (NT - turn) % NT, 0)
 
 
 def update_kernel(

time: 131 us -> 131 us (level)
    all_to_all x4, blocking collectives: 86.9 us -> 84.8 us  [swap_rows(): y = lax.all_to_all(x.reshape(NT, LEG, 1, CELLS), 'inst', 0, 0, tiled=True)]
where the time goes in v6:
time: 131 us; the launch traced here: 130 us
  blocking collectives  116 us (89%)
  Pallas kernels  13.9 us (11%)
    all_to_all x4, blocking collectives, swap_rows(): y = lax.all_to_all(x.reshape(NT, LEG, 1, CELLS), 'inst', 0, 0, tiled=True)  84.8 us
    all_to_all x2, blocking collectives, swap(): lax.all_to_all(x.reshape(parts, rows // parts, CELLS), axis, 0, 0, tiled=...  30.7 us
    pallas_call x2, Pallas kernels, per_device(): pl.pallas_call(lambda *refs, sweep=sweep: mix_kernel(STALL[sweep], *refs)...  8.98 us

profile of v6, /device:TPU:6, one launch (start us, length us, event | category | flops | bytes accessed | tf_op | source)
XLA Modules:
  0.0 129.9 jit_solution(17998203652611095817)
XLA Ops:
  0.0 0.1 pad_add_fusion.place.refs_3_.inst.refs_4_
  0.1 0.0 copy-start
  0.1 0.0 copy-start.2
  0.1 0.0 copy-start.3
  0.1 0.0 copy-start.4
  0.2 0.0 copy-start.5
  0.2 0.0 copy-start.6
  0.2 0.0 copy-start.7
  0.2 0.0 copy-start.8
  0.2 1.2 pack.1
  1.4 16.6 %all_to_all.30 = f32[32,24,128]{2,1,0:T(8,128)S(1)} all-to-all(f32[32,24,128]{2,1,0:T(8,128)S(1)} %bitcast.31), channel_id=1, replica_groups=mesh['inst'=16,'mesh'=32] {'mesh'}, dimensions={0} | all-to-all | bytes 786432 | tf_op jit(solution)/shard_map/all_to_all | solution.py:168
  18.1 0.0 copy-done
  18.1 0.0 copy-done.2
  18.1 0.0 copy-done.3
  18.1 0.0 copy-done.4
  18.1 0.0 copy-done.5
  18.1 0.0 copy-done.6
  18.1 0.0 copy-done.7
  18.2 0.0 copy-done.8
  18.2 0.0 copy-start.11
  18.2 4.9 %mix.2 = (f32[400,128]{1,0:T(8,128)S(1)}, f32[384,128]{1,0:T(8,128)S(1)}, f32[64,128]{1,0:T(8,128)S(1)}) custom-call(f32[400,128]{1,0:T(8,128)S(1)} %broadcast_in_dim.9.refs_0_, s32[2,2]{1,0:T(2,128)S(1)} %copy-done.7, f32[2,2]{1,0:T(2,128)S(1)} %copy-done.8, ...), custom_call_target="tpu_custom_call", output_to_operand_aliasing={{0}: (0, {}), {1}: (11, {}), {2}: (12, {})} | custom-call | tf_op jit(solution)/shard_map/mix/pallas_call | solution.py:224
  23.0 0.0 copy-start.1
  23.1 0.0 copy-start.9
  23.1 0.0 copy-start.10
  23.1 27.9 %all_to_all.31 = f32[16,25,1,128]{3,2,1,0:T(1,128)S(1)} all-to-all(f32[16,25,1,128]{3,2,1,0:T(1,128)S(1)} %bitcast.39), channel_id=1, replica_groups=mesh['inst'=16,'mesh'=32] {'inst'}, dimensions={0} | all-to-all | bytes 409600 | tf_op jit(solution)/shard_map/all_to_all | solution.py:173
  50.9 0.0 copy-done.11
  50.9 0.7 spectral.2
  51.6 18.2 %all_to_all.32 = f32[16,25,1,128]{3,2,1,0:T(1,128)S(1)} all-to-all(f32[16,25,1,128]{3,2,1,0:T(1,128)S(1)} %bitcast.41), channel_id=1, replica_groups=mesh['inst'=16,'mesh'=32] {'inst'}, dimensions={0} | all-to-all | bytes 409600 | tf_op jit(solution)/shard_map/all_to_all | solution.py:173
  69.8 0.0 copy-done.1
  69.9 0.0 copy-done.9
  69.9 0.0 copy-done.10
  69.9 1.0 update.2
  70.9 14.1 %all_to_all.33 = f32[32,24,128]{2,1,0:T(8,128)S(1)} all-to-all(f32[32,24,128]{2,1,0:T(8,128)S(1)} %bitcast.26), channel_id=1, replica_groups=mesh['inst'=16,'mesh'=32] {'mesh'}, dimensions={0} | all-to-all | bytes 786432 | tf_op jit(solution)/shard_map/all_to_all | solution.py:168
  85.0 4.1 %mix.3 = (f32[400,128]{1,0:T(8,128)S(1)}, f32[384,128]{1,0:T(8,128)S(1)}, f32[64,128]{1,0:T(8,128)S(1)}) custom-call(f32[400,128]{1,0:T(8,128)S(1)} %bitcast.33, s32[2,2]{1,0:T(2,128)S(1)} %copy-done.7, f32[2,2]{1,0:T(2,128)S(1)} %copy-done.8, ...), custom_call_target="tpu_custom_call", output_to_operand_aliasing={{0}: (0, {}), {1}: (11, {}), {2}: (12, {})} | custom-call | tf_op jit(solution)/shard_map/mix/pallas_call | solution.py:224
  89.1 20.2 %all_to_all.34 = f32[16,25,1,128]{3,2,1,0:T(1,128)S(1)} all-to-all(f32[16,25,1,128]{3,2,1,0:T(1,128)S(1)} %bitcast.34), channel_id=1, replica_groups=mesh['inst'=16,'mesh'=32] {'inst'}, dimensions={0} | all-to-all | bytes 409600 | tf_op jit(solution)/shard_map/all_to_all | solution.py:173
  109.3 0.7 spectral.3
  110.0 18.5 %all_to_all.35 = f32[16,25,1,128]{3,2,1,0:T(1,128)S(1)} all-to-all(f32[16,25,1,128]{3,2,1,0:T(1,128)S(1)} %bitcast.43), channel_id=1, replica_groups=mesh['inst'=16,'mesh'=32] {'inst'}, dimensions={0} | all-to-all | bytes 409600 | tf_op jit(solution)/shard_map/all_to_all | solution.py:173
  128.5 1.4 %update.3 = f32[384,128]{1,0:T(8,128)} custom-call(f32[384,128]{1,0:T(8,128)S(1)} %get-tuple-element.18.refs_0_, f32[64,128]{1,0:T(8,128)S(1)} %get-tuple-element.19.refs_1_, f32[2304,128]{1,0:T(8,128)S(1)} %bitcast.28, f32[2,128]{1,0:T(2,128)S(1)} %copy-done.9, s32[2]{0:T(128)S(1)} %pad_add_fusion.place.refs_3_.inst.refs_4_, f32[400,128]{1,0:T(8,128)S(1)} %bitcast.47, ...), custom_call_target="tpu_custom_call" | custom-call | tf_op jit(solution)/shard_map/update/pallas_call | solution.py:254
  (5 shorter events, 0.1 us)
Async XLA Ops:
  0.1 18.0 %copy-start = (f32[3,1,6,64,128]{4,3,2,1,0:T(8,128)S(1)}, f32[3,1,6,64,128]{4,3,2,1,0:T(8,128)}, u32[]{:S(2)}) copy-start(f32[3,1,6,64,128]{4,3,2,1,0:T(8,128)} %param.14) | copy-start | bytes 1769476
  0.1 18.0 %copy-start.2 = (f32[1,6,64,128]{3,2,1,0:T(8,128)S(1)}, f32[1,6,64,128]{3,2,1,0:T(8,128)}, u32[]{:S(2)}) copy-start(f32[1,6,64,128]{3,2,1,0:T(8,128)} %param.13) | copy-start | bytes 589828
  0.1 18.0 %copy-start.3 = (f32[1,6,64,128]{3,2,1,0:T(8,128)S(1)}, f32[1,6,64,128]{3,2,1,0:T(8,128)}, u32[]{:S(2)}) copy-start(f32[1,6,64,128]{3,2,1,0:T(8,128)} %param.12) | copy-start | bytes 589828
  0.1 18.0 %copy-start.4 = (f32[64,128]{1,0:T(8,128)S(1)}, f32[64,128]{1,0:T(8,128)}, u32[]{:S(2)}) copy-start(f32[64,128]{1,0:T(8,128)} %refs_9_.7) | copy-start | bytes 98308
  0.2 18.0 %copy-start.5 = (s32[64]{0:T(128)S(1)}, s32[64]{0:T(128)}, u32[]{:S(2)}) copy-start(s32[64]{0:T(128)} %refs_10_.3) | copy-start | bytes 772
  0.2 18.0 %copy-start.6 = (s32[64]{0:T(128)S(1)}, s32[64]{0:T(128)}, u32[]{:S(2)}) copy-start(s32[64]{0:T(128)} %refs_11_.3) | copy-start | bytes 772
  0.2 18.0 %copy-start.7 = (s32[2,2]{1,0:T(2,128)S(1)}, s32[2,2]{1,0:T(2,128)}, u32[]{:S(2)}) copy-start(s32[2,2]{1,0:T(2,128)} %refs_1_.3) | copy-start | bytes 52
  0.2 18.0 %copy-start.8 = (f32[2,2]{1,0:T(2,128)S(1)}, f32[2,2]{1,0:T(2,128)}, u32[]{:S(2)}) copy-start(f32[2,2]{1,0:T(2,128)} %refs_2_.3) | copy-start | bytes 52
  18.2 32.8 %copy-start.11 = (s32[2]{0:T(128)S(1)}, s32[2]{0:T(128)}, u32[]{:S(2)}) copy-start(s32[2]{0:T(128)} %shift.3) | copy-start | bytes 28
  23.0 46.8 %copy-start.1 = (f32[1,6,6,64,128]{4,3,2,1,0:T(8,128)S(1)}, f32[1,6,6,64,128]{4,3,2,1,0:T(8,128)}, u32[]{:S(2)}) copy-start(f32[1,6,6,64,128]{4,3,2,1,0:T(8,128)} %param.15) | copy-start | bytes 3538948
  23.1 46.8 %copy-start.9 = (f32[2,128]{1,0:T(2,128)S(1)}, f32[2,128]{1,0:T(2,128)}, u32[]{:S(2)}) copy-start(f32[2,128]{1,0:T(2,128)} %refs_3_.3) | copy-start | bytes 3076
  23.1 46.8 %copy-start.10 = (s32[32,2]{0,1:T(2,128)S(1)}, s32[32,2]{0,1:T(2,128)}, u32[]{:S(2)}) copy-start(s32[32,2]{0,1:T(2,128)} %param.18) | copy-start | bytes 772

commit v7 on v6

--- a/solution.py
+++ b/solution.py
@@ -45,7 +45,8 @@
             out[pl.ds(dst * SLOT + (2 + b) * NV, NV), :] = faces[b]
 
 
-def pack_kernel(field, send, place, out_in, out):
+def pack_kernel(field, send, shift, place, out_in, turn_in, out, turn):
+    turn[...] = jnp.full((NT, CELLS), jnp.where(place[0] < NV, shift[0], shift[1]), jnp.int32)
     pack_blocks(field, send, out)
 
 
@@ -91,7 +92,7 @@
         spin[...] = lax.fori_loop(0, stall, lambda i, x: pltpu.roll(x, 1, 1), field[pl.ds(0, 8), :])
 
 
-def spectral_kernel(legs, shift, inst, out):
+def spectral_kernel(legs, turn, out):
     half = NT // 2
     for t in range(PIECE // 8):
         rows = [legs[pl.ds(m * LEG + t * 8, 8), :] for m in range(NT)]
@@ -105,9 +106,10 @@
                 b = b + minus[m] * ODD[(n - m) % NT]
             out[pl.ds(n * LEG + t * 8, 8), :] = a + b
             out[pl.ds((n + half) * LEG + t * 8, 8), :] = a - b
-    turn = jnp.where(inst[0] < NV, shift[0], shift[1])
     mixes = legs[pl.ds(PIECE, NT, stride=LEG), :]
-    out[pl.ds(PIECE, NT, stride=LEG), :] = pltpu.roll(mixes, (NT - turn) % NT, 0)
+    for bit in (1, 2, 4, 8):
+        mixes = jnp.where((turn[...] & bit) > 0, pltpu.roll(mixes, NT - bit, 0), mixes)
+    out[pl.ds(PIECE, NT, stride=LEG), :] = mixes
 
 
 def update_kernel(
@@ -203,15 +205,22 @@
     recv = recv_slot
     blade = row_id
 
-    packed = pl.pallas_call(
+    packed, turn = pl.pallas_call(
         pack_kernel,
-        out_shape=rows_of(NMESH * SLOT),
-        in_specs=[vmem(), smem(), smem(), vmem()],
-        out_specs=vmem(),
-        input_output_aliases={3: 0},
+        out_shape=[rows_of(NMESH * SLOT), jax.ShapeDtypeStruct((NT, CELLS), jnp.int32)],
+        in_specs=[vmem(), smem(), smem(), smem(), vmem(), vmem()],
+        out_specs=[vmem()] * 2,
+        input_output_aliases={4: 0, 5: 1},
         name="pack",
         compiler_params=pltpu.CompilerParams(vmem_limit_bytes=8 << 20),
-    )(far(field), far(send), place, near(jnp.zeros((NMESH * SLOT, CELLS), F32)))
+    )(
+        far(field),
+        far(send),
+        far(shift),
+        place,
+        near(jnp.zeros((NMESH * SLOT, CELLS), F32)),
+        near(jnp.zeros((NT, CELLS), jnp.int32)),
+    )
     fresh = jnp.zeros((ROWS, CELLS), F32)
     part = jnp.zeros((ROWS, CELLS), F32)
     freq = jnp.zeros((BLK, CELLS), F32)
@@ -235,12 +244,12 @@
         back = pl.pallas_call(
             spectral_kernel,
             out_shape=rows_of(NT * LEG),
-            in_specs=[vmem(), smem(), smem()],
+            in_specs=[vmem(), vmem()],
             out_specs=vmem(),
             input_output_aliases={0: 0},
             name="spectral",
             compiler_params=pltpu.CompilerParams(vmem_limit_bytes=8 << 20),
-        )(legs, shift, place)
+        )(legs, near(turn))
         back = near(swap_rows(back))
         ins = [near(part), near(freq), jac, iface_coef, place, back] + near_by
         specs = [vmem()] * 4 + [smem(), vmem()] + near_specs

time: 131 us -> 130 us (level)
  no operation moved by 1% of the time
where the time goes in v7:
time: 130 us; the launch traced here: 129 us
  blocking collectives  116 us (89%)
  Pallas kernels  12.9 us (10%)
    all_to_all x4, blocking collectives, swap_rows(): y = lax.all_to_all(x.reshape(NT, LEG, 1, CELLS), 'inst', 0, 0, tiled=True)  84.9 us
    all_to_all x2, blocking collectives, swap(): lax.all_to_all(x.reshape(parts, rows // parts, CELLS), axis, 0, 0, tiled=...  30.7 us
    pallas_call x2, Pallas kernels, per_device(): pl.pallas_call(lambda *refs, sweep=sweep: mix_kernel(STALL[sweep], *refs)...  8.97 us

profile of v7, /device:TPU:6, one launch (start us, length us, event | category | flops | bytes accessed | tf_op | source)
XLA Modules:
  0.0 128.9 jit_solution(9831876527898361718)
XLA Ops:
  0.0 0.0 copy-start.3
  0.0 0.0 copy-start.6
  0.0 0.0 copy-start.5
  0.0 0.0 copy-start.4
  0.0 0.0 copy-start.9
  0.0 0.0 copy-start.8
  0.0 0.0 copy-start
  0.0 0.0 copy-start.2
  0.1 0.1 pad_add_fusion.place.refs_3_.refs_4_
  0.2 1.4 %pack.1 = (f32[768,128]{1,0:T(8,128)S(1)}, s32[16,128]{1,0:T(8,128)S(1)}) custom-call(f32[384,128]{1,0:T(8,128)} %bitcast.44, s32[2,32]{1,0:T(2,128)} %bitcast.48, s32[2]{0:T(128)} %shift.1, s32[2]{0:T(128)S(1)} %pad_add_fusion.place.refs_3_.refs_4_, f32[768,128]{1,0:T(8,128)S(1)} %broadcast_in_dim.13.out_in, ...), custom_call_target="tpu_custom_call", output_to_operand_aliasing={{0}: (4, {}), {1}: (5, {})} | custom-call | tf_op jit(solution)/shard_map/pack/pallas_call | solution.py:208
  1.5 16.6 %all_to_all.30 = f32[32,24,128]{2,1,0:T(8,128)S(1)} all-to-all(f32[32,24,128]{2,1,0:T(8,128)S(1)} %bitcast.31), channel_id=1, replica_groups=mesh['inst'=16,'mesh'=32] {'mesh'}, dimensions={0} | all-to-all | bytes 786432 | tf_op jit(solution)/shard_map/all_to_all | solution.py:170
  18.2 0.0 copy-done.3
  18.2 0.0 copy-done.6
  18.2 0.0 copy-done.5
  18.2 0.0 copy-done.4
  18.2 0.0 copy-done.9
  18.2 0.0 copy-done.8
  18.2 0.0 copy-done
  18.2 0.0 copy-done.2
  18.2 4.9 %mix.2 = (f32[400,128]{1,0:T(8,128)S(1)}, f32[384,128]{1,0:T(8,128)S(1)}, f32[64,128]{1,0:T(8,128)S(1)}) custom-call(f32[400,128]{1,0:T(8,128)S(1)} %broadcast_in_dim.12.refs_0_, s32[2,2]{1,0:T(2,128)S(1)} %copy-done.8, f32[2,2]{1,0:T(2,128)S(1)} %copy-done.9, ...), custom_call_target="tpu_custom_call", output_to_operand_aliasing={{0}: (0, {}), {1}: (11, {}), {2}: (12, {})} | custom-call | tf_op jit(solution)/shard_map/mix/pallas_call | solution.py:233
  23.1 0.0 copy-start.1
  23.1 0.0 copy-start.7
  23.1 0.0 copy-start.10
  23.1 27.9 %all_to_all.31 = f32[16,25,1,128]{3,2,1,0:T(1,128)S(1)} all-to-all(f32[16,25,1,128]{3,2,1,0:T(1,128)S(1)} %bitcast.39), channel_id=1, replica_groups=mesh['inst'=16,'mesh'=32] {'inst'}, dimensions={0} | all-to-all | bytes 409600 | tf_op jit(solution)/shard_map/all_to_all | solution.py:175
  51.0 0.1 spectral.2
  51.1 18.2 %all_to_all.32 = f32[16,25,1,128]{3,2,1,0:T(1,128)S(1)} all-to-all(f32[16,25,1,128]{3,2,1,0:T(1,128)S(1)} %bitcast.41), channel_id=1, replica_groups=mesh['inst'=16,'mesh'=32] {'inst'}, dimensions={0} | all-to-all | bytes 409600 | tf_op jit(solution)/shard_map/all_to_all | solution.py:175
  69.4 0.0 copy-done.1
  69.4 0.0 copy-done.7
  69.4 0.0 copy-done.10
  69.4 1.0 update.2
  70.4 14.1 %all_to_all.33 = f32[32,24,128]{2,1,0:T(8,128)S(1)} all-to-all(f32[32,24,128]{2,1,0:T(8,128)S(1)} %bitcast.26), channel_id=1, replica_groups=mesh['inst'=16,'mesh'=32] {'mesh'}, dimensions={0} | all-to-all | bytes 786432 | tf_op jit(solution)/shard_map/all_to_all | solution.py:170
  84.5 4.1 %mix.3 = (f32[400,128]{1,0:T(8,128)S(1)}, f32[384,128]{1,0:T(8,128)S(1)}, f32[64,128]{1,0:T(8,128)S(1)}) custom-call(f32[400,128]{1,0:T(8,128)S(1)} %bitcast.33, s32[2,2]{1,0:T(2,128)S(1)} %copy-done.8, f32[2,2]{1,0:T(2,128)S(1)} %copy-done.9, s32[2]{0:T(128)S(1)} %pad_add_fusion.place.refs_3_.refs_4_, ...), custom_call_target="tpu_custom_call", output_to_operand_aliasing={{0}: (0, {}), {1}: (11, {}), {2}: (12, {})} | custom-call | tf_op jit(solution)/shard_map/mix/pallas_call | solution.py:233
  88.6 20.2 %all_to_all.34 = f32[16,25,1,128]{3,2,1,0:T(1,128)S(1)} all-to-all(f32[16,25,1,128]{3,2,1,0:T(1,128)S(1)} %bitcast.34), channel_id=1, replica_groups=mesh['inst'=16,'mesh'=32] {'inst'}, dimensions={0} | all-to-all | bytes 409600 | tf_op jit(solution)/shard_map/all_to_all | solution.py:175
  108.9 0.1 spectral.3
  109.0 18.5 %all_to_all.35 = f32[16,25,1,128]{3,2,1,0:T(1,128)S(1)} all-to-all(f32[16,25,1,128]{3,2,1,0:T(1,128)S(1)} %bitcast.43), channel_id=1, replica_groups=mesh['inst'=16,'mesh'=32] {'inst'}, dimensions={0} | all-to-all | bytes 409600 | tf_op jit(solution)/shard_map/all_to_all | solution.py:175
  127.5 1.4 %update.3 = f32[384,128]{1,0:T(8,128)} custom-call(f32[384,128]{1,0:T(8,128)S(1)} %get-tuple-element.22.refs_0_, f32[64,128]{1,0:T(8,128)S(1)} %get-tuple-element.23.refs_1_, f32[2304,128]{1,0:T(8,128)S(1)} %bitcast.28, f32[2,128]{1,0:T(2,128)S(1)} %copy-done.10, s32[2]{0:T(128)S(1)} %pad_add_fusion.place.refs_3_.refs_4_, f32[400,128]{1,0:T(8,128)S(1)} %bitcast.47, ...), custom_call_target="tpu_custom_call" | custom-call | tf_op jit(solution)/shard_map/update/pallas_call | solution.py:263
  (6 shorter events, 0.1 us)
Async XLA Ops:
  0.0 18.2 %copy-start.3 = (f32[1,6,64,128]{3,2,1,0:T(8,128)S(1)}, f32[1,6,64,128]{3,2,1,0:T(8,128)}, u32[]{:S(2)}) copy-start(f32[1,6,64,128]{3,2,1,0:T(8,128)} %param.12) | copy-start | bytes 589828
  0.0 18.2 %copy-start.6 = (s32[64]{0:T(128)S(1)}, s32[64]{0:T(128)}, u32[]{:S(2)}) copy-start(s32[64]{0:T(128)} %refs_11_.3) | copy-start | bytes 772
  0.0 18.2 %copy-start.5 = (s32[64]{0:T(128)S(1)}, s32[64]{0:T(128)}, u32[]{:S(2)}) copy-start(s32[64]{0:T(128)} %refs_10_.3) | copy-start | bytes 772
  0.0 18.2 %copy-start.4 = (f32[64,128]{1,0:T(8,128)S(1)}, f32[64,128]{1,0:T(8,128)}, u32[]{:S(2)}) copy-start(f32[64,128]{1,0:T(8,128)} %refs_9_.7) | copy-start | bytes 98308
  0.0 18.2 %copy-start.9 = (f32[2,2]{1,0:T(2,128)S(1)}, f32[2,2]{1,0:T(2,128)}, u32[]{:S(2)}) copy-start(f32[2,2]{1,0:T(2,128)} %refs_2_.3) | copy-start | bytes 52
  0.0 18.2 %copy-start.8 = (s32[2,2]{1,0:T(2,128)S(1)}, s32[2,2]{1,0:T(2,128)}, u32[]{:S(2)}) copy-start(s32[2,2]{1,0:T(2,128)} %refs_1_.3) | copy-start | bytes 52
  0.0 18.2 %copy-start = (f32[3,1,6,64,128]{4,3,2,1,0:T(8,128)S(1)}, f32[3,1,6,64,128]{4,3,2,1,0:T(8,128)}, u32[]{:S(2)}) copy-start(f32[3,1,6,64,128]{4,3,2,1,0:T(8,128)} %param.14) | copy-start | bytes 1769476
  0.0 18.2 %copy-start.2 = (f32[1,6,64,128]{3,2,1,0:T(8,128)S(1)}, f32[1,6,64,128]{3,2,1,0:T(8,128)}, u32[]{:S(2)}) copy-start(f32[1,6,64,128]{3,2,1,0:T(8,128)} %param.13) | copy-start | bytes 589828
  23.1 46.3 %copy-start.1 = (f32[1,6,6,64,128]{4,3,2,1,0:T(8,128)S(1)}, f32[1,6,6,64,128]{4,3,2,1,0:T(8,128)}, u32[]{:S(2)}) copy-start(f32[1,6,6,64,128]{4,3,2,1,0:T(8,128)} %param.15) | copy-start | bytes 3538948
  23.1 46.3 %copy-start.7 = (s32[32,2]{0,1:T(2,128)S(1)}, s32[32,2]{0,1:T(2,128)}, u32[]{:S(2)}) copy-start(s32[32,2]{0,1:T(2,128)} %param.18) | copy-start | bytes 772
  23.1 46.3 %copy-start.10 = (f32[2,128]{1,0:T(2,128)S(1)}, f32[2,128]{1,0:T(2,128)}, u32[]{:S(2)}) copy-start(f32[2,128]{1,0:T(2,128)} %refs_3_.3) | copy-start | bytes 3076

commit v8 on v7

--- a/solution.py
+++ b/solution.py
@@ -16,7 +16,7 @@
 SLOT = 4 * NV
 LEG = PIECE + 1
 SWEEPS = 2
-STALL = (700, 560)
+STALL = (620, 560)
 F32 = jnp.float32
 
 
@@ -70,7 +70,7 @@
 
 
 def mix_kernel(
-    stall, legs, donor, weight, place, field, right, coup, spec, row_id, recv, blocks, part_in, freq_in,
+    stall, last, legs, donor, weight, place, field, right, coup, spec, row_id, recv, blocks, part_in, freq_in,
     out, part, freq, halo, spin,
 ):
     for p in range(NT):
@@ -86,9 +86,12 @@
             total = face if total is None else total + face
         for v in range(NV):
             out[pl.ds((j * NV + v) * LEG + PIECE, 1), :] = total[v : v + 1]
+    @pl.when((place[1] % 2 == 0) | last)
+    def _():
+        local_terms(field, right, coup, spec, row_id, recv, blocks, part, freq, halo)
+
     @pl.when(place[1] % 2 == 0)
     def _():
-        local_terms(field, right, coup, spec, row_id, recv, blocks, part, freq, halo)
         spin[...] = lax.fori_loop(0, stall, lambda i, x: pltpu.roll(x, 1, 1), field[pl.ds(0, 8), :])
 
 
@@ -112,22 +115,24 @@
     out[pl.ds(PIECE, NT, stride=LEG), :] = mixes
 
 
-def update_kernel(
-    last, part_in, freq_in, jac, coef, place, back, field, right, coup, spec, row_id, recv, blocks, *rest
-):
+def update_kernel(last, part_in, freq_in, jac, coef, *rest):
     if last:
-        out, part, freq, halo = rest
+        back, out, part, freq, halo = rest
+        part, freq = part_in, freq_in
     else:
-        send, fresh, out, packed, part, freq, halo = rest
-
-    @pl.when(place[1] % 2 == 0)
-    def _():
-        part[...] = part_in[...]
-        freq[...] = freq_in[...]
-
-    @pl.when(place[1] % 2 == 1)
-    def _():
-        local_terms(field, right, coup, spec, row_id, recv, blocks, part, freq, halo)
+        (
+            place, back, field, right, coup, spec, row_id, recv, blocks,
+            send, fresh, out, packed, part, freq, halo,
+        ) = rest
+
+        @pl.when(place[1] % 2 == 0)
+        def _():
+            part[...] = part_in[...]
+            freq[...] = freq_in[...]
+
+        @pl.when(place[1] % 2 == 1)
+        def _():
+            local_terms(field, right, coup, spec, row_id, recv, blocks, part, freq, halo)
 
     sub = lax.broadcasted_iota(jnp.int32, (8, CELLS), 0)
     for t in range(BLK // 8):
@@ -231,7 +236,7 @@
         near_by = [near(field), right, coup, spec, blade, recv, blocks]
         near_specs = [vmem(), vmem(), vmem(), vmem(), smem(), smem(), vmem()]
         legs, part, freq = pl.pallas_call(
-            lambda *refs, sweep=sweep: mix_kernel(STALL[sweep], *refs),
+            lambda *refs, sweep=sweep: mix_kernel(STALL[sweep], sweep == SWEEPS - 1, *refs),
             out_shape=[rows_of(NT * LEG), rows_of(ROWS), rows_of(BLK)],
             in_specs=[vmem(), smem(), smem(), smem()] + near_specs + [vmem()] * 2,
             out_specs=[vmem()] * 3,
@@ -260,6 +265,8 @@
             specs += [smem(), vmem()]
             shapes.append(rows_of(NMESH * SLOT))
             alias = {14: 0, 12: 1}
+        if last:
+            ins, specs = ins[:4] + [back], [vmem()] * 5
         res = pl.pallas_call(
             lambda *refs, last=last: update_kernel(last, *refs),
             out_shape=shapes,

time: 130 us -> 130 us (level)
    all_to_all x4, blocking collectives: 84.9 us -> 86.9 us  [swap_rows(): y = lax.all_to_all(x.reshape(NT, LEG, 1, CELLS), 'inst', 0, 0, tiled=True)]
where the time goes in v8:
time: 130 us; the launch traced here: 129 us
  blocking collectives  117 us (90%)
  Pallas kernels  12 us (9%)
    all_to_all x4, blocking collectives, swap_rows(): y = lax.all_to_all(x.reshape(NT, LEG, 1, CELLS), 'inst', 0, 0, tiled=True)  86.9 us
    all_to_all x2, blocking collectives, swap(): lax.all_to_all(x.reshape(parts, rows // parts, CELLS), axis, 0, 0, tiled=...  29.8 us
    pallas_call x2, Pallas kernels, per_device(): pl.pallas_call(lambda *refs, sweep=sweep: mix_kernel(STALL[sweep], sweep...  8.56 us

profile of v8, /device:TPU:6, one launch (start us, length us, event | category | flops | bytes accessed | tf_op | source)
XLA Modules:
  0.0 129.1 jit_solution(1810189664767225485)
XLA Ops:
  0.0 0.0 copy-start.3
  0.0 0.0 copy-start.6
  0.0 0.0 copy-start.5
  0.0 0.0 copy-start.4
  0.0 0.0 copy-start.9
  0.0 0.0 copy-start.8
  0.0 0.0 copy-start
  0.0 0.0 copy-start.2
  0.1 0.1 pad_add_fusion.place.refs_3_.refs_4_
  0.2 1.4 %pack.1 = (f32[768,128]{1,0:T(8,128)S(1)}, s32[16,128]{1,0:T(8,128)S(1)}) custom-call(f32[384,128]{1,0:T(8,128)} %bitcast.40, s32[2,32]{1,0:T(2,128)} %bitcast.45, s32[2]{0:T(128)} %shift.1, s32[2]{0:T(128)S(1)} %pad_add_fusion.place.refs_3_.refs_4_, f32[768,128]{1,0:T(8,128)S(1)} %broadcast_in_dim.13.out_in, ...), custom_call_target="tpu_custom_call", output_to_operand_aliasing={{0}: (4, {}), {1}: (5, {})} | custom-call | tf_op jit(solution)/shard_map/pack/pallas_call | solution.py:213
  1.5 16.6 %all_to_all.30 = f32[32,24,128]{2,1,0:T(8,128)S(1)} all-to-all(f32[32,24,128]{2,1,0:T(8,128)S(1)} %bitcast.28), channel_id=1, replica_groups=mesh['inst'=16,'mesh'=32] {'mesh'}, dimensions={0} | all-to-all | bytes 786432 | tf_op jit(solution)/shard_map/all_to_all | solution.py:175
  18.2 0.0 copy-done.3
  18.2 0.0 copy-done.6
  18.2 0.0 copy-done.5
  18.2 0.0 copy-done.4
  18.2 0.0 copy-done.9
  18.2 0.0 copy-done.8
  18.2 0.0 copy-done
  18.2 0.0 copy-done.2
  18.2 4.4 %mix.2 = (f32[400,128]{1,0:T(8,128)S(1)}, f32[384,128]{1,0:T(8,128)S(1)}, f32[64,128]{1,0:T(8,128)S(1)}) custom-call(f32[400,128]{1,0:T(8,128)S(1)} %broadcast_in_dim.12.refs_0_, s32[2,2]{1,0:T(2,128)S(1)} %copy-done.8, f32[2,2]{1,0:T(2,128)S(1)} %copy-done.9, ...), custom_call_target="tpu_custom_call", output_to_operand_aliasing={{0}: (0, {}), {1}: (11, {}), {2}: (12, {})} | custom-call | tf_op jit(solution)/shard_map/mix/pallas_call | solution.py:238
  22.7 0.0 copy-start.1
  22.7 0.0 copy-start.7
  22.7 0.0 copy-start.10
  22.7 29.4 %all_to_all.31 = f32[16,25,1,128]{3,2,1,0:T(1,128)S(1)} all-to-all(f32[16,25,1,128]{3,2,1,0:T(1,128)S(1)} %bitcast.32), channel_id=1, replica_groups=mesh['inst'=16,'mesh'=32] {'inst'}, dimensions={0} | all-to-all | bytes 409600 | tf_op jit(solution)/shard_map/all_to_all | solution.py:180
  52.1 0.1 spectral.2
  52.2 19.1 %all_to_all.32 = f32[16,25,1,128]{3,2,1,0:T(1,128)S(1)} all-to-all(f32[16,25,1,128]{3,2,1,0:T(1,128)S(1)} %bitcast.34), channel_id=1, replica_groups=mesh['inst'=16,'mesh'=32] {'inst'}, dimensions={0} | all-to-all | bytes 409600 | tf_op jit(solution)/shard_map/all_to_all | solution.py:180
  71.3 0.0 copy-done.1
  71.3 0.0 copy-done.7
  71.3 0.0 copy-done.10
  71.3 1.0 update.2
  72.3 13.2 %all_to_all.33 = f32[32,24,128]{2,1,0:T(8,128)S(1)} all-to-all(f32[32,24,128]{2,1,0:T(8,128)S(1)} %bitcast.22), channel_id=1, replica_groups=mesh['inst'=16,'mesh'=32] {'mesh'}, dimensions={0} | all-to-all | bytes 786432 | tf_op jit(solution)/shard_map/all_to_all | solution.py:175
  85.6 4.1 %mix.3 = (f32[400,128]{1,0:T(8,128)S(1)}, f32[384,128]{1,0:T(8,128)S(1)}, f32[64,128]{1,0:T(8,128)S(1)}) custom-call(f32[400,128]{1,0:T(8,128)S(1)} %bitcast.30, s32[2,2]{1,0:T(2,128)S(1)} %copy-done.8, f32[2,2]{1,0:T(2,128)S(1)} %copy-done.9, s32[2]{0:T(128)S(1)} %pad_add_fusion.place.refs_3_.refs_4_, ...), custom_call_target="tpu_custom_call", output_to_operand_aliasing={{0}: (0, {}), {1}: (11, {}), {2}: (12, {})} | custom-call | tf_op jit(solution)/shard_map/mix/pallas_call | solution.py:238
  89.7 18.7 %all_to_all.34 = f32[16,25,1,128]{3,2,1,0:T(1,128)S(1)} all-to-all(f32[16,25,1,128]{3,2,1,0:T(1,128)S(1)} %bitcast.31), channel_id=1, replica_groups=mesh['inst'=16,'mesh'=32] {'inst'}, dimensions={0} | all-to-all | bytes 409600 | tf_op jit(solution)/shard_map/all_to_all | solution.py:180
  108.4 0.1 spectral.3
  108.5 19.7 %all_to_all.35 = f32[16,25,1,128]{3,2,1,0:T(1,128)S(1)} all-to-all(f32[16,25,1,128]{3,2,1,0:T(1,128)S(1)} %bitcast.36), channel_id=1, replica_groups=mesh['inst'=16,'mesh'=32] {'inst'}, dimensions={0} | all-to-all | bytes 409600 | tf_op jit(solution)/shard_map/all_to_all | solution.py:180
  128.2 0.8 update.3
  (6 shorter events, 0.1 us)
Async XLA Ops:
  0.0 18.2 %copy-start.3 = (f32[1,6,64,128]{3,2,1,0:T(8,128)S(1)}, f32[1,6,64,128]{3,2,1,0:T(8,128)}, u32[]{:S(2)}) copy-start(f32[1,6,64,128]{3,2,1,0:T(8,128)} %param.12) | copy-start | bytes 589828
  0.0 18.2 %copy-start.6 = (s32[64]{0:T(128)S(1)}, s32[64]{0:T(128)}, u32[]{:S(2)}) copy-start(s32[64]{0:T(128)} %refs_9_.5) | copy-start | bytes 772
  0.0 18.2 %copy-start.5 = (s32[64]{0:T(128)S(1)}, s32[64]{0:T(128)}, u32[]{:S(2)}) copy-start(s32[64]{0:T(128)} %refs_8_.3) | copy-start | bytes 772
  0.0 18.2 %copy-start.4 = (f32[64,128]{1,0:T(8,128)S(1)}, f32[64,128]{1,0:T(8,128)}, u32[]{:S(2)}) copy-start(f32[64,128]{1,0:T(8,128)} %refs_7_.3) | copy-start | bytes 98308
  0.0 18.2 %copy-start.9 = (f32[2,2]{1,0:T(2,128)S(1)}, f32[2,2]{1,0:T(2,128)}, u32[]{:S(2)}) copy-start(f32[2,2]{1,0:T(2,128)} %refs_2_.3) | copy-start | bytes 52
  0.0 18.2 %copy-start.8 = (s32[2,2]{1,0:T(2,128)S(1)}, s32[2,2]{1,0:T(2,128)}, u32[]{:S(2)}) copy-start(s32[2,2]{1,0:T(2,128)} %refs_1_.3) | copy-start | bytes 52
  0.0 18.2 %copy-start = (f32[3,1,6,64,128]{4,3,2,1,0:T(8,128)S(1)}, f32[3,1,6,64,128]{4,3,2,1,0:T(8,128)}, u32[]{:S(2)}) copy-start(f32[3,1,6,64,128]{4,3,2,1,0:T(8,128)} %param.14) | copy-start | bytes 1769476
  0.0 18.2 %copy-start.2 = (f32[1,6,64,128]{3,2,1,0:T(8,128)S(1)}, f32[1,6,64,128]{3,2,1,0:T(8,128)}, u32[]{:S(2)}) copy-start(f32[1,6,64,128]{3,2,1,0:T(8,128)} %param.13) | copy-start | bytes 589828
  22.7 48.6 %copy-start.1 = (f32[1,6,6,64,128]{4,3,2,1,0:T(8,128)S(1)}, f32[1,6,6,64,128]{4,3,2,1,0:T(8,128)}, u32[]{:S(2)}) copy-start(f32[1,6,6,64,128]{4,3,2,1,0:T(8,128)} %param.15) | copy-start | bytes 3538948
  22.7 48.6 %copy-start.7 = (s32[32,2]{0,1:T(2,128)S(1)}, s32[32,2]{0,1:T(2,128)}, u32[]{:S(2)}) copy-start(s32[32,2]{0,1:T(2,128)} %param.18) | copy-start | bytes 772
  22.7 48.6 %copy-start.10 = (f32[2,128]{1,0:T(2,128)S(1)}, f32[2,128]{1,0:T(2,128)}, u32[]{:S(2)}) copy-start(f32[2,128]{1,0:T(2,128)} %refs_3_.3) | copy-start | bytes 3076
